TPU v7x, 32 devices: a whole 2x2x4 slice. The times are simulated.
32 devices in a mesh: lat: 4 (over y, x), lon: 8 (over z, core).
Axes of the slice: x: 2, y: 2, z: 4, core: 2. Of those that a mesh axis runs over, the one named last changes fastest.
Arguments:
- forcing: float32 [2, 2, 8, 64, 64], P(None, None, None, 'lat', 'lon'), may hold values from -6 to 6
- zonal: float32 [8, 64, 64], P(None, 'lat', 'lon'), may hold values from -0.3 to 0.3
- meridional: float32 [8, 64, 64], P(None, 'lat', 'lon'), may hold values from -0.3 to 0.3
- mixing: float32 [7, 64, 64], P(None, 'lat', 'lon'), may hold values from 0.03 to 0.24
- panel: bfloat16 [4096, 4, 1024], P('lat', None, 'lon'), may hold values from -0.125 to 0.125
Outputs:
- adjoint_state: float32 [2, 8, 64, 64], P(None, None, 'lat', 'lon')
- state_grad: float32 [2, 8, 4, 1024], P(None, None, 'lat', 'lon')
- flux_grad: float32 [2, 4, 1024], P(None, 'lat', 'lon')
All inputs are finite; a program needn't handle non-finite values.
Results may differ from a plain program's by a relative error of at most 0.0029.
Values may be sent and summed in bfloat16 or wider, within the bound.
No kernel may reach another device: no remote copies, remote signals or barrier semaphores. Data moves between devices by JAX's collectives and lax.ppermute only.
A program may use at most 64 MiB of HBM per device.

v0:
```python
import jax
import jax.numpy as jnp
from jax import lax
from jax.sharding import PartitionSpec as P


def extended(value, sides, width, wrap):
    for axis, dim in sides:
        peers, length = (lax.axis_size(axis), value.shape[dim])
        up = [(i, (i + 1) % peers) for i in range(peers if wrap else peers - 1)]
        down = [(j, i) for i, j in up]
        last = lax.slice_in_dim(value, length - width, length, axis=dim)
        initial = lax.slice_in_dim(value, 0, width, axis=dim)
        before = lax.ppermute(last, axis, up)
        after = lax.ppermute(initial, axis, down)
        value = jnp.concatenate([before, value, after], axis=dim)
    return value


def diffuse(tracer, mixing):
    flow = mixing * (tracer[..., 1:, :, :] - tracer[..., :-1, :, :])
    zeros = jnp.zeros_like(flow[..., :1, :, :])
    return tracer + jnp.concatenate([flow, zeros], -3) - jnp.concatenate([zeros, flow], -3)


def advect_local(tracer, zonal_ext, merid_ext):
    centre = tracer[..., 1:-1, 1:-1]
    out_east = jnp.maximum(zonal_ext[:, 1:-1, 1:-1], 0.0)
    in_west = jnp.minimum(zonal_ext[:, 1:-1, :-2], 0.0)
    out_north = jnp.maximum(merid_ext[:, 1:-1, 1:-1], 0.0)
    in_south = jnp.minimum(merid_ext[:, :-2, 1:-1], 0.0)
    return (
        centre * (1.0 - out_east + in_west - out_north + in_south)
        + tracer[..., 1:-1, 2:] * out_east
        - tracer[..., 1:-1, :-2] * in_west
        + tracer[..., 2:, 1:-1] * out_north
        - tracer[..., :-2, 1:-1] * in_south
    )


def widen(planes):
    widened = extended(planes, (("lon", 2),), 1, True)
    return extended(widened, (("lat", 1),), 1, False)


def row_adder(panel, piece):
    return jnp.einsum("rc,cam->ram", piece, panel, preferred_element_type=jnp.float32)


def precondition(vectors, panel):
    total = row_adder(panel, lax.all_gather(vectors, "lon", axis=1, tiled=True))
    return lax.psum_scatter(total, "lat", scatter_dimension=1, tiled=True)


def shards(forcing, zonal, meridional, mixing, panel):
    levels, band_rows, band_cols = zonal.shape
    cell_count = band_rows * band_cols
    row_index = lax.axis_index("lat") * band_rows + jnp.arange(band_rows, dtype=jnp.int32)
    total_rows = band_rows * lax.axis_size("lat")
    top_mask = (row_index < total_rows - 1).astype(jnp.float32)[None, :, None]
    merid_masked = meridional * top_mask
    started = diffuse(forcing[1], mixing).reshape(2 * levels, band_rows, band_cols)
    widened = widen(jnp.concatenate([started, zonal, merid_masked], 0))
    costate_ext = widened[: 2 * levels].reshape(2, levels, band_rows + 2, band_cols + 2)
    zonal_ext = widened[2 * levels : 3 * levels]
    merid_ext = widened[3 * levels :]
    middle = advect_local(costate_ext, zonal_ext, merid_ext) + forcing[0]
    surface = forcing[1][:, 0] + middle[:, 0]
    flux_vec = surface.reshape(2, cell_count).astype(jnp.bfloat16)
    mixed = diffuse(middle, mixing).reshape(2 * levels, band_rows, band_cols)
    mixed_ext = widen(mixed).reshape(2, levels, band_rows + 2, band_cols + 2)
    adjoint_state = advect_local(mixed_ext, zonal_ext, merid_ext)
    state_vec = adjoint_state.reshape(2 * levels, cell_count).astype(jnp.bfloat16)
    summed = precondition(jnp.concatenate([flux_vec, state_vec], 0), panel)
    flux_grad = summed[:2]
    state_grad = summed[2:].reshape(2, levels, summed.shape[1], summed.shape[2])
    return (adjoint_state, state_grad, flux_grad)


def solution(mesh):
    return jax.shard_map(
        shards,
        mesh=mesh,
        in_specs=(
            P(None, None, None, "lat", "lon"),
            P(None, "lat", "lon"),
            P(None, "lat", "lon"),
            P(None, "lat", "lon"),
            P("lat", None, "lon"),
        ),
        out_specs=(P(None, None, "lat", "lon"), P(None, None, "lat", "lon"), P(None, "lat", "lon")),
        check_vma=False,
    )
```

profile of v0, /device:TPU:0, one launch (start us, length us, event | category | flops | bytes accessed | tf_op | source)
XLA Modules:
  0.0 69.0 jit_solution(5245259998162481026)
XLA Ops:
  0.6 0.0 copy-start
  0.7 0.0 copy-start.3
  0.7 0.9 %slice_bitcast_fusion = f32[2,8,16,8]{2,3,1,0:T(8,128)S(1)} fusion(f32[2,2,8,16,8]{3,4,2,1,0:T(8,128)} %param.5), kind=kLoop, calls=%fused_computation.33 | loop fusion | bytes 16384 | tf_op jit(solution)/shard_map/squeeze | solution.py:62
  1.6 0.0 copy-done.3
  1.6 0.0 copy-start.1
  1.6 0.9 %copy-done.1 = f32[2,2,8,16,8]{3,4,2,1,0:T(8,128)S(1)} copy-done((f32[2,2,8,16,8]{3,4,2,1,0:T(8,128)S(1)}, f32[2,2,8,16,8]{3,4,2,1,0:T(8,128)}, u32[]{:S(2)}) %copy-start.1) | copy-done | bytes 16408
  2.5 0.0 copy-start.4
  2.5 0.7 %copy-done.4 = f32[8,16,8]{1,2,0:T(8,128)S(1)} copy-done((f32[8,16,8]{1,2,0:T(8,128)S(1)}, f32[8,16,8]{1,2,0:T(8,128)}, u32[]{:S(2)}) %copy-start.4) | copy-done | bytes 4120
  3.3 0.0 copy-start.2
  3.3 0.7 %copy-done.2 = f32[8,16,8]{1,2,0:T(8,128)S(1)} copy-done((f32[8,16,8]{1,2,0:T(8,128)S(1)}, f32[8,16,8]{1,2,0:T(8,128)}, u32[]{:S(2)}) %copy-start.2) | copy-done | bytes 4120
  4.1 0.5 collective-permute-start
  4.6 4.1 %collective-permute-start.1 = (f32[32,16,1]{1,2,0:T(1,128)S(1)}, f32[32,16,1]{1,2,0:T(1,128)S(1)}, u32[]{:S(2)}, u32[]{:S(2)}) collective-permute-start(f32[32,16,1]{1,2,0:T(1,128)S(1)} %get-tuple-element.27), channel_id=1, source_target_pairs={{1,0},{2,1},{3,2},{4,3},{5,4},{6,5},{7,6},{0,7},{9,8},{10,9},{11,1... | collective-permute-start | bytes 6152 | tf_op jit(solution)/shard_map/ppermute | solution.py:15
  8.7 0.1 copy.56
  8.8 1.3 %collective-permute-done = f32[32,16,1]{1,2,0:T(1,128)S(1)} collective-permute-done((f32[32,16,1]{1,2,0:T(1,128)S(1)}, f32[32,16,1]{1,2,0:T(1,128)S(1)}, u32[]{:S(2)}, u32[]{:S(2)}) %collective-permute-start) | collective-permute-done | bytes 2080 | tf_op jit(solution)/shard_map/ppermute | solution.py:14
  10.1 0.1 copy.55
  10.1 0.0 collective-permute-done.1
  10.2 0.1 copy.57
  10.2 3.9 %collective-permute-start.2 = (f32[32,1,10]{0,1,2:T(1,128)S(1)}, f32[32,1,10]{0,1,2:T(1,128)S(1)}, u32[]{:S(2)}, u32[]{:S(2)}) collective-permute-start(f32[32,1,10]{0,1,2:T(1,128)S(1)} %get-tuple-element.34), channel_id=1, source_target_pairs={{0,8},{8,16},{16,24},{1,9},{9,17},{17,25},{2,10},{10,18},{18,26},{... | collective-permute-start | bytes 3848 | tf_op jit(solution)/shard_map/ppermute | solution.py:14
  14.1 1.3 %collective-permute-start.3 = (f32[32,1,10]{0,1,2:T(1,128)S(1)}, f32[32,1,10]{0,1,2:T(1,128)S(1)}, u32[]{:S(2)}, u32[]{:S(2)}) collective-permute-start(f32[32,1,10]{0,1,2:T(1,128)S(1)} %get-tuple-element.33), channel_id=1, source_target_pairs={{8,0},{16,8},{24,16},{9,1},{17,9},{25,17},{10,2},{18,10},{26,18},{... | collective-permute-start | bytes 3848 | tf_op jit(solution)/shard_map/ppermute | solution.py:15
  15.4 0.0 collective-permute-done.2
  15.5 0.1 pad_maximum_fusion.7
  15.6 0.1 copy.72
  15.6 4.0 %collective-permute-done.3 = f32[32,1,10]{0,1,2:T(1,128)S(1)} collective-permute-done((f32[32,1,10]{0,1,2:T(1,128)S(1)}, f32[32,1,10]{0,1,2:T(1,128)S(1)}, u32[]{:S(2)}, u32[]{:S(2)}) %collective-permute-start.3) | collective-permute-done | bytes 1312 | tf_op jit(solution)/shard_map/ppermute | solution.py:15
  19.7 0.1 copy.70
  19.8 0.1 fusion.21
  20.0 0.1 fusion.7
  20.2 0.1 collective-permute-start.4
  20.2 3.5 %collective-permute-start.5 = (f32[16,16,1]{1,2,0:T(1,128)S(1)}, f32[16,16,1]{1,2,0:T(1,128)S(1)}, u32[]{:S(2)}, u32[]{:S(2)}) collective-permute-start(f32[16,16,1]{1,2,0:T(1,128)S(1)} %get-tuple-element.36), channel_id=1, source_target_pairs={{1,0},{2,1},{3,2},{4,3},{5,4},{6,5},{7,6},{0,7},{9,8},{10,9},{11,1... | collective-permute-start | bytes 3080 | tf_op jit(solution)/shard_map/ppermute | solution.py:15
  23.8 0.0 copy-start.5
  23.8 0.7 copy-done.5
  24.4 0.7 dynamic-slice
  25.1 0.0 collective-permute-done.4
  25.1 0.0 collective-permute-done.5
  25.2 0.1 fusion.19
  25.3 4.3 %collective-permute-start.6 = (f32[16,1,10]{1,2,0:T(8,128)S(1)}, f32[16,1,10]{1,2,0:T(8,128)S(1)}, u32[]{:S(2)}, u32[]{:S(2)}) collective-permute-start(f32[16,1,10]{1,2,0:T(8,128)S(1)} %get-tuple-element.24), channel_id=1, source_target_pairs={{0,8},{8,16},{16,24},{1,9},{9,17},{17,25},{2,10},{10,18},{18,26},{... | collective-permute-start | bytes 1928 | tf_op jit(solution)/shard_map/ppermute | solution.py:14
  29.6 1.3 %collective-permute-start.7 = (f32[16,1,10]{1,2,0:T(8,128)S(1)}, f32[16,1,10]{1,2,0:T(8,128)S(1)}, u32[]{:S(2)}, u32[]{:S(2)}) collective-permute-start(f32[16,1,10]{1,2,0:T(8,128)S(1)} %get-tuple-element.25), channel_id=1, source_target_pairs={{8,0},{16,8},{24,16},{9,1},{17,9},{25,17},{10,2},{18,10},{26,18},{... | collective-permute-start | bytes 1928 | tf_op jit(solution)/shard_map/ppermute | solution.py:15
  30.9 0.1 copy.65
  31.0 0.1 convert_element_type.21
  31.1 1.0 %collective-permute-done.6 = f32[16,1,10]{1,2,0:T(8,128)S(1)} collective-permute-done((f32[16,1,10]{1,2,0:T(8,128)S(1)}, f32[16,1,10]{1,2,0:T(8,128)S(1)}, u32[]{:S(2)}, u32[]{:S(2)}) %collective-permute-start.6) | collective-permute-done | bytes 672 | tf_op jit(solution)/shard_map/ppermute | solution.py:14
  32.1 4.4 %collective-permute-done.7 = f32[16,1,10]{1,2,0:T(8,128)S(1)} collective-permute-done((f32[16,1,10]{1,2,0:T(8,128)S(1)}, f32[16,1,10]{1,2,0:T(8,128)S(1)}, u32[]{:S(2)}, u32[]{:S(2)}) %collective-permute-start.7) | collective-permute-done | bytes 672 | tf_op jit(solution)/shard_map/ppermute | solution.py:15
  36.5 0.2 pad_maximum_fusion.2
  36.6 0.8 %fusion.16 = (bf16[2,8,16,8]{2,3,1,0:T(8,128)(2,1)S(1)}, f32[2,8,16,8]{2,3,1,0:T(8,128)}) fusion(f32[8,16,8]{1,2,0:T(8,128)S(1)} %get-tuple-element.38, f32[2,8,18,10]{2,3,1,0:T(8,128)S(1)} %bitcast.26, f32[8,16,8]{1,2,0:T(8,128)S(1)} %get-tuple-element.22, f32[8,16,8]{1,2,0:T(8,128)S(1)} %get-tuple-element.21, f32[8,16,8]{1,2,0:T(8,128)S(1)} %get-tuple-element.37, ...), kind=kLoop, calls=%fused_computation.57 | loop fusion | flops 20480 | bytes 73728 | tf_op jit(solution)/shard_map/convert_element_type | solution.py:73
  37.4 0.1 copy.66
  37.5 0.1 convert_element_type.23
  37.6 12.7 %all_gather.3 = bf16[18,1024]{1,0:T(8,128)(2,1)S(1)} all-gather(bf16[18,128]{1,0:T(8,128)(2,1)S(1)} %pad_maximum_fusion.13), channel_id=1, replica_groups=mesh['lat'=4,'lon'=8] {'lon'}, dimensions={1}, use_global_device_ids=true | all-gather | bytes 41472 | tf_op jit(solution)/shard_map/all_gather | solution.py:51
  50.4 0.0 copy-done
  50.4 0.3 fusion
  50.6 15.8 %all-reduce.4 = f32[18,4,128]{2,0,1:T(8,128)S(1)} all-reduce(f32[18,4,128]{2,0,1:T(8,128)S(1)} %fusion), channel_id=2, replica_groups=mesh['lat'=4,'lon'=8] {'lat'}, use_global_device_ids=true, to_apply=%region_0.0.clone | all-reduce | flops 9216 | bytes 73728
  66.5 1.3 %constant_dynamic-slice_fusion.1 = f32[2,1,128]{2,0,1:T(2,128)} fusion(f32[18,4,128]{2,0,1:T(8,128)S(1)} %all-reduce.4, u32[]{:T(128)} %bitcast.10), kind=kLoop, calls=%fused_computation.56 | loop fusion | bytes 2052 | tf_op jit(solution)/shard_map/slice | solution.py:75
  67.7 1.3 %constant_dynamic-slice_fusion = f32[16,1,128]{2,0,1:T(8,128)} fusion(f32[18,4,128]{2,0,1:T(8,128)S(1)} %all-reduce.4, u32[]{:T(128)S(6)} %convert, u32[]{:T(128)} %bitcast.10), kind=kLoop, calls=%fused_computation.55 | loop fusion | bytes 16392 | tf_op jit(solution)/shard_map/slice | solution.py:76
  (15 shorter events, 0.2 us)
Async XLA Ops:
  0.6 49.7 %copy-start = (bf16[1024,4,128]{2,1,0:T(4,128)(2,1)S(1)}, bf16[1024,4,128]{2,1,0:T(4,128)(2,1)}, u32[]{:S(2)}) copy-start(bf16[1024,4,128]{2,1,0:T(4,128)(2,1)} %param.9) | copy-start | bytes 3145732
  0.7 0.9 %copy-start.3 = (f32[7,16,8]{1,2,0:T(8,128)S(1)}, f32[7,16,8]{1,2,0:T(8,128)}, u32[]{:S(2)}) copy-start(f32[7,16,8]{1,2,0:T(8,128)} %param.8) | copy-start | bytes 10756
  1.6 0.9 %copy-start.1 = (f32[2,2,8,16,8]{3,4,2,1,0:T(8,128)S(1)}, f32[2,2,8,16,8]{3,4,2,1,0:T(8,128)}, u32[]{:S(2)}) copy-start(f32[2,2,8,16,8]{3,4,2,1,0:T(8,128)} %param.5) | copy-start | bytes 49156
  2.5 0.8 %copy-start.4 = (f32[8,16,8]{1,2,0:T(8,128)S(1)}, f32[8,16,8]{1,2,0:T(8,128)}, u32[]{:S(2)}) copy-start(f32[8,16,8]{1,2,0:T(8,128)} %param.7) | copy-start | bytes 12292
  3.3 0.8 %copy-start.2 = (f32[8,16,8]{1,2,0:T(8,128)S(1)}, f32[8,16,8]{1,2,0:T(8,128)}, u32[]{:S(2)}) copy-start(f32[8,16,8]{1,2,0:T(8,128)} %param.6) | copy-start | bytes 12292
  4.1 6.0 %collective-permute-start = (f32[32,16,1]{1,2,0:T(1,128)S(1)}, f32[32,16,1]{1,2,0:T(1,128)S(1)}, u32[]{:S(2)}, u32[]{:S(2)}) collective-permute-start(f32[32,16,1]{1,2,0:T(1,128)S(1)} %get-tuple-element.26), channel_id=1, source_target_pairs={{0,1},{1,2},{2,3},{3,4},{4,5},{5,6},{6,7},{7,0},{8,9},{9,10},{10,1... | collective-permute-start | bytes 6152 | tf_op jit(solution)/shard_map/ppermute | solution.py:14
  4.6 5.5 %collective-permute-start.1 = (f32[32,16,1]{1,2,0:T(1,128)S(1)}, f32[32,16,1]{1,2,0:T(1,128)S(1)}, u32[]{:S(2)}, u32[]{:S(2)}) collective-permute-start(f32[32,16,1]{1,2,0:T(1,128)S(1)} %get-tuple-element.27), channel_id=1, source_target_pairs={{1,0},{2,1},{3,2},{4,3},{5,4},{6,5},{7,6},{0,7},{9,8},{10,9},{11,1... | collective-permute-start | bytes 6152 | tf_op jit(solution)/shard_map/ppermute | solution.py:15
  10.2 5.2 %collective-permute-start.2 = (f32[32,1,10]{0,1,2:T(1,128)S(1)}, f32[32,1,10]{0,1,2:T(1,128)S(1)}, u32[]{:S(2)}, u32[]{:S(2)}) collective-permute-start(f32[32,1,10]{0,1,2:T(1,128)S(1)} %get-tuple-element.34), channel_id=1, source_target_pairs={{0,8},{8,16},{16,24},{1,9},{9,17},{17,25},{2,10},{10,18},{18,26},{... | collective-permute-start | bytes 3848 | tf_op jit(solution)/shard_map/ppermute | solution.py:14
  14.1 5.5 %collective-permute-start.3 = (f32[32,1,10]{0,1,2:T(1,128)S(1)}, f32[32,1,10]{0,1,2:T(1,128)S(1)}, u32[]{:S(2)}, u32[]{:S(2)}) collective-permute-start(f32[32,1,10]{0,1,2:T(1,128)S(1)} %get-tuple-element.33), channel_id=1, source_target_pairs={{8,0},{16,8},{24,16},{9,1},{17,9},{25,17},{10,2},{18,10},{26,18},{... | collective-permute-start | bytes 3848 | tf_op jit(solution)/shard_map/ppermute | solution.py:15
  20.2 4.9 %collective-permute-start.4 = (f32[16,16,1]{1,2,0:T(1,128)S(1)}, f32[16,16,1]{1,2,0:T(1,128)S(1)}, u32[]{:S(2)}, u32[]{:S(2)}) collective-permute-start(f32[16,16,1]{1,2,0:T(1,128)S(1)} %get-tuple-element.35), channel_id=1, source_target_pairs={{0,1},{1,2},{2,3},{3,4},{4,5},{5,6},{6,7},{7,0},{8,9},{9,10},{10,1... | collective-permute-start | bytes 3080 | tf_op jit(solution)/shard_map/ppermute | solution.py:14
  20.2 4.9 %collective-permute-start.5 = (f32[16,16,1]{1,2,0:T(1,128)S(1)}, f32[16,16,1]{1,2,0:T(1,128)S(1)}, u32[]{:S(2)}, u32[]{:S(2)}) collective-permute-start(f32[16,16,1]{1,2,0:T(1,128)S(1)} %get-tuple-element.36), channel_id=1, source_target_pairs={{1,0},{2,1},{3,2},{4,3},{5,4},{6,5},{7,6},{0,7},{9,8},{10,9},{11,1... | collective-permute-start | bytes 3080 | tf_op jit(solution)/shard_map/ppermute | solution.py:15
  23.8 0.7 copy-start.5
  25.3 6.8 %collective-permute-start.6 = (f32[16,1,10]{1,2,0:T(8,128)S(1)}, f32[16,1,10]{1,2,0:T(8,128)S(1)}, u32[]{:S(2)}, u32[]{:S(2)}) collective-permute-start(f32[16,1,10]{1,2,0:T(8,128)S(1)} %get-tuple-element.24), channel_id=1, source_target_pairs={{0,8},{8,16},{16,24},{1,9},{9,17},{17,25},{2,10},{10,18},{18,26},{... | collective-permute-start | bytes 1928 | tf_op jit(solution)/shard_map/ppermute | solution.py:14
  29.6 6.9 %collective-permute-start.7 = (f32[16,1,10]{1,2,0:T(8,128)S(1)}, f32[16,1,10]{1,2,0:T(8,128)S(1)}, u32[]{:S(2)}, u32[]{:S(2)}) collective-permute-start(f32[16,1,10]{1,2,0:T(8,128)S(1)} %get-tuple-element.25), channel_id=1, source_target_pairs={{8,0},{16,8},{24,16},{9,1},{17,9},{25,17},{10,2},{18,10},{26,18},{... | collective-permute-start | bytes 1928 | tf_op jit(solution)/shard_map/ppermute | solution.py:15
where the time goes:
time: 69.4 us; the launch traced here: 69 us
  blocking collectives  28.6 us (41%)
  starting transfers between devices  19 us (27%)
  waiting for transfers between devices  10.7 us (15%)
  local copies, waits for them, and re-layouts  8.29 us (12%)
  other arithmetic  1.35 us (2%)
  between operations  0.84 us (1%)
    unnamed x1, blocking collectives  15.8 us
    all_gather x1, blocking collectives, precondition(): total = row_adder(panel, lax.all_gather(vectors, 'lon', axis=1, tiled=True))  12.7 us
    ppermute x4, starting transfers between devices, extended(): after = lax.ppermute(initial, axis, down)  10.2 us
    ppermute x4, starting transfers between devices, extended(): before = lax.ppermute(last, axis, up)  8.8 us
    ppermute x4, waiting for transfers between devices, extended(): after = lax.ppermute(initial, axis, down)  8.44 us
    unnamed x15, local copies, waits for them, and re-layouts  3.92 us
    ppermute x4, waiting for transfers between devices, extended(): before = lax.ppermute(last, axis, up)  2.29 us
  transfers between devices with their start and end apart: 8, of which 4 were waited for; matrix products, arithmetic and copies ran while one was open for 2% of the time, Pallas kernels for 0%

commit v1 on v0

v1 whole, which is shorter than its diff:
```python
import functools
import jax
import jax.numpy as jnp
from jax import lax
from jax.experimental import pallas as pl
from jax.experimental.pallas import tpu as pltpu
from jax.sharding import PartitionSpec as P

DIRECT = 4


def roll(value, shift, axis=-1):
    axis %= value.ndim
    return pltpu.roll(value, shift % value.shape[axis], axis)


def band_kernel(rows, cols, blocks, exchanged, band_ref, vec_ref, adjoint_ref, all_ref):
    me = lax.axis_index("lon")
    cells = rows * cols
    two = 2 * cols

    def load(block):
        if exchanged:
            apart = jnp.bitwise_xor(block, me)
            place = (apart % 2) * (blocks // 2) + apart // 2
        else:
            place = block
        return band_ref[place]

    loaded = [load(block) for block in range(blocks)]

    def field(start, count):
        return jnp.stack([block[start : start + 8 * count].reshape(count, 8, cells) for block in loaded])

    forced, first, zonal, merid, mixing, halo = (
        field(0, 2), field(16, 2), field(32, 1), field(40, 1), field(48, 1), field(56, 2))
    lane = lax.broadcasted_iota(jnp.int32, (1, 1, 8, cells), 3)
    column = lane % cols

    def tile(main, source, place):
        beyond = roll(source, two - place * 2 * two)
        return jnp.where(lane < two, roll(main, two), jnp.where(lane < 3 * two, beyond, roll(main, 3 * two)))

    def rotated(value, by):
        return jnp.concatenate([value[by:], value[:by]], 0)

    def east(value):
        return jnp.where(column == cols - 1, roll(rotated(value, 1), cols - 1), roll(value, -1))

    def west(value):
        return jnp.where(column == 0, roll(rotated(value, -1), 1 - cols), roll(value, 1))

    def north(value, edge=None):
        moved = roll(value, -cols)
        return moved if edge is None else jnp.where(lane >= cells - cols, roll(edge, -3 * cols), moved)

    def south(value, edge=None):
        moved = roll(value, cols)
        return moved if edge is None else jnp.where(lane < cols, roll(edge, -5 * cols), moved)

    def diffuse(value, mix):
        flow = mix * (roll(value, -1, -2) - value)
        return value + flow - roll(flow, 1, -2)

    def factors(across, along, edge=None):
        out_east = jnp.maximum(across, 0.0)
        in_west = jnp.minimum(west(across), 0.0)
        out_north = jnp.maximum(along, 0.0)
        in_south = jnp.minimum(south(along, edge), 0.0)
        return (1.0 - out_east + in_west - out_north + in_south, out_east, in_west, out_north, in_south)

    def advect(value, factor, edge=None):
        centre, out_east, in_west, out_north, in_south = factor
        return (value * centre + east(value) * out_east - west(value) * in_west
                + north(value, edge) * out_north - south(value, edge) * in_south)

    forced_tile = tile(forced, halo, 0)
    first_tile = tile(first, halo, 1)
    zonal_tile = tile(zonal, halo[:, :1], 2)
    mixing_tile = tile(mixing, halo[:, 1:], 2)
    merid_tile = tile(merid, halo[:, :1], 3)
    main_factor = factors(zonal, merid, merid_tile)
    tile_factor = factors(zonal_tile, merid_tile)
    started = diffuse(forced, mixing)
    started_tile = diffuse(forced_tile, mixing_tile)
    middle = advect(started, main_factor, started_tile) + first
    middle_tile = advect(started_tile, tile_factor) + first_tile
    mixed = diffuse(middle, mixing)
    mixed_tile = diffuse(middle_tile, mixing_tile)
    adjoint = advect(mixed, main_factor, mixed_tile)
    surface = forced + middle
    for block in range(blocks):
        span = slice(block * cells, (block + 1) * cells)
        own = adjoint[block].reshape(16, cells)
        all_ref[block] = own
        vec_ref[:16, span] = own.astype(jnp.bfloat16)
        pair = jnp.concatenate([surface[block, 0, :1], surface[block, 1, :1]], 0)
        vec_ref[16:18, span] = pair.astype(jnp.bfloat16)
    adjoint_ref[...] = all_ref[me]


def band_vectors(band, rows, cols, blocks, exchanged):
    cells = rows * cols
    return pl.pallas_call(
        functools.partial(band_kernel, rows, cols, blocks, exchanged),
        out_shape=(jax.ShapeDtypeStruct((18, blocks * cells), jnp.bfloat16), jax.ShapeDtypeStruct((16, cells), jnp.float32)),
        in_specs=[pl.BlockSpec(memory_space=pltpu.VMEM)],
        out_specs=(pl.BlockSpec(memory_space=pltpu.VMEM), pl.BlockSpec(memory_space=pltpu.VMEM)),
        scratch_shapes=[pltpu.VMEM((blocks, 16, cells), jnp.float32)],
        name="band",
    )(band)


def swapped(value, axis, apart):
    peers = lax.axis_size(axis)
    return lax.ppermute(value, axis, [(i, i ^ apart) for i in range(peers) if i ^ apart < peers])


def along_lat(upper, lower):
    peers = lax.axis_size("lat")
    even = lax.axis_index("lat") % 2 == 0
    pairs = [(i, i ^ 1) for i in range(peers)]
    others = [(i, i + 1 if i % 2 else i - 1) for i in range(1, peers - 1)]
    nearer = lax.ppermute(jnp.where(even, upper, lower), "lat", pairs)
    farther = lax.ppermute(jnp.where(even, lower, upper), "lat", others)
    return nearer + farther


def gathered(packed):
    peers = lax.axis_size("lon")
    if peers > 2 * DIRECT:
        return lax.all_gather(packed, "lon", axis=0), False
    pieces = [packed] + [swapped(packed, "lon", apart) for apart in range(2, peers, 2)]
    own = jnp.stack(pieces)
    return jnp.concatenate([own, swapped(own, "lon", 1)], 0), True


def scattered(total):
    peers = lax.axis_size("lat")
    if peers > DIRECT:
        return lax.psum_scatter(total, "lat", scatter_dimension=1, tiled=True)
    me = lax.axis_index("lat")
    kept = lax.dynamic_slice_in_dim(total, me, 1, 1)
    for apart in range(1, peers):
        piece = lax.dynamic_slice_in_dim(total, me ^ apart, 1, 1)
        kept = kept + swapped(piece, "lat", apart)
    return kept


def shards(forcing, zonal, meridional, mixing, panel):
    levels, rows, cols = zonal.shape
    cells = rows * cols
    row_index = lax.axis_index("lat") * rows + jnp.arange(rows, dtype=jnp.int32)
    below_top = row_index < rows * lax.axis_size("lat") - 1
    masked = jnp.where(below_top[None, :, None], meridional, 0.0)
    forced = forcing[1].reshape(2 * levels, cells)
    first = forcing[0].reshape(2 * levels, cells)
    across = zonal.reshape(levels, cells)
    along = masked.reshape(levels, cells)
    mixed = jnp.concatenate([mixing.reshape(levels - 1, cells), jnp.zeros((1, cells), jnp.float32)], 0)
    pair = jnp.concatenate([across, mixed], 0)
    lone = jnp.concatenate([along, jnp.zeros_like(along)], 0)
    two = 2 * cols
    blank = jnp.zeros((2 * levels, two), jnp.float32)
    sources = (forced, first, pair, lone)
    upper = jnp.concatenate([piece for s in sources for piece in (blank, s[:, cells - two :])], 1)
    lower = jnp.concatenate([piece for s in sources for piece in (s[:, :two], blank)], 1)
    halo = along_lat(upper, lower)
    packed = jnp.concatenate([forced, first, across, along, mixed, halo], 0)
    band, exchanged = gathered(packed)
    vectors, adjoint = band_vectors(band, rows, cols, lax.axis_size("lon"), exchanged)
    total = jnp.einsum("rc,cam->ram", vectors, panel, preferred_element_type=jnp.float32)
    summed = scattered(total)
    state_grad = summed[:16].reshape(2, levels, 1, summed.shape[2])
    flux_grad = summed[16:]
    return (adjoint.reshape(2, levels, rows, cols), state_grad, flux_grad)


def solution(mesh):
    return jax.shard_map(
        shards,
        mesh=mesh,
        in_specs=(
            P(None, None, None, "lat", "lon"),
            P(None, "lat", "lon"),
            P(None, "lat", "lon"),
            P(None, "lat", "lon"),
            P("lat", None, "lon"),
        ),
        out_specs=(P(None, None, "lat", "lon"), P(None, None, "lat", "lon"), P(None, "lat", "lon")),
        check_vma=False,
    )
```

time: 69.4 us -> 37.4 us (0.54)
  blocking collectives: 28.6 us -> 0 us
  starting transfers between devices: 19 us -> 15.8 us
  Pallas kernels: 0 us -> 2.34 us
  local copies, waits for them, and re-layouts: 8.29 us -> 6.91 us
  other arithmetic: 1.35 us -> 0.05 us
  waiting for transfers between devices: 10.7 us -> 9.89 us
  matrix products: 0.25 us -> 1.05 us
    unnamed x1 -> x0, blocking collectives: 15.8 us -> none
    all_gather x1 -> x0, blocking collectives: 12.7 us -> none  [precondition(): total = row_adder(panel, lax.all_gather(vectors, 'lon', axis=1, tiled=True))]
    ppermute x8 -> x9, starting transfers between devices: 19 us -> 15.8 us  [the longest x7 12.1 us: swapped(): lax.ppermute(value, axis, [(i, i ^ apart) for i in range(peers) if i ^ ap...]
    pallas_call x0 -> x1, Pallas kernels: none -> 2.34 us  [band_vectors(): pl.pallas_call(functools.partial(band_kernel, rows, cols, blocks, exchang...]
    squeeze x1 -> x0, local copies, waits for them, and re-layouts: 0.93 us -> none  [shards(): forcing[1]]
    ppermute x8 -> x9, waiting for transfers between devices: 10.7 us -> 9.89 us  [the longest x7 8.93 us: swapped(): lax.ppermute(value, axis, [(i, i ^ apart) for i in range(peers) if i ^ ap...]
    dot_general x1, matrix products: 0.25 us -> 1.05 us  [shards(): jnp.einsum('rc,cam->ram', vectors, panel, preferred_element_type=jnp.floa...]
    convert_element_type x3 -> x0, other arithmetic: 0.78 us -> none  [the longest x1 0.77 us: shards(): adjoint_state.reshape(2 * levels, cell_count).astype(jnp.bfloat16)]
  transfers between devices with their start and end apart: 8 -> 9, of which waited for: 4 -> 5; matrix products, arithmetic and copies ran while one was open for 2% -> 2% of each run, Pallas kernels for 0% -> 0%
where the time goes in v1:
time: 37.4 us; the launch traced here: 36.9 us
  starting transfers between devices  15.8 us (42%)
  waiting for transfers between devices  9.89 us (26%)
  local copies, waits for them, and re-layouts  6.91 us (18%)
  Pallas kernels  2.34 us (6%)
  matrix products  1.05 us (3%)
  between operations  0.86 us (2%)
    ppermute x7, starting transfers between devices, swapped(): lax.ppermute(value, axis, [(i, i ^ apart) for i in range(peers) if i ^ ap...  12.1 us
    ppermute x7, waiting for transfers between devices, swapped(): lax.ppermute(value, axis, [(i, i ^ apart) for i in range(peers) if i ^ ap...  8.93 us
    unnamed x19, local copies, waits for them, and re-layouts  3.56 us
    ppermute x1, starting transfers between devices, along_lat(): nearer = lax.ppermute(jnp.where(even, upper, lower), 'lat', pairs)  3.03 us
    pallas_call x1, Pallas kernels, band_vectors(): pl.pallas_call(functools.partial(band_kernel, rows, cols, blocks, exchang...  2.34 us
    slice x2, local copies, waits for them, and re-layouts, shards(): first = forcing[0].reshape(2 * levels, cells)  1.06 us
    dot_general x1, matrix products, shards(): jnp.einsum('rc,cam->ram', vectors, panel, preferred_element_type=jnp.floa...  1.05 us
    ppermute x1, waiting for transfers between devices, along_lat(): nearer = lax.ppermute(jnp.where(even, upper, lower), 'lat', pairs)  0.95 us
  transfers between devices with their start and end apart: 9, of which 5 were waited for; matrix products, arithmetic and copies ran while one was open for 2% of the time, Pallas kernels for 0%

profile of v1, /device:TPU:0, one launch (start us, length us, event | category | flops | bytes accessed | tf_op | source)
XLA Modules:
  0.0 36.9 jit_solution(16146679234065082166)
XLA Ops:
  0.6 0.0 copy-start
  0.7 1.0 %fusion.3 = (f32[1,2,8,16,8]{3,4,2,1,0:T(8,128)S(1)}, f32[1,2,8,16,8]{3,4,2,1,0:T(8,128)S(1)}) fusion(f32[2,2,8,16,8]{3,4,2,1,0:T(8,128)} %param.5), kind=kLoop, calls=%fused_computation.20 | loop fusion | bytes 32768 | tf_op jit(solution)/shard_map/slice | solution.py:157
  1.6 0.1 copy.17
  1.7 0.1 reshape_squeeze.6
  1.8 0.1 copy.18
  1.9 0.0 copy-start.2
  1.9 0.1 reshape_squeeze.7
  2.1 0.6 %copy-done.2 = f32[8,16,8]{1,2,0:T(8,128)S(1)} copy-done((f32[8,16,8]{1,2,0:T(8,128)S(1)}, f32[8,16,8]{1,2,0:T(8,128)}, u32[]{:S(2)}) %copy-start.2) | copy-done | bytes 4120
  2.7 0.1 copy.19
  2.8 0.0 copy-start.3
  2.8 0.1 reshape.26
  2.9 0.6 %copy-done.3 = f32[8,16,8]{1,2,0:T(8,128)S(1)} copy-done((f32[8,16,8]{1,2,0:T(8,128)S(1)}, f32[8,16,8]{1,2,0:T(8,128)}, u32[]{:S(2)}) %copy-start.3) | copy-done | bytes 4120
  3.5 0.1 copy.20
  3.6 0.0 copy-start.4
  3.6 0.1 reshape.27
  3.7 0.7 %copy-done.4 = f32[7,16,8]{1,2,0:T(8,128)S(1)} copy-done((f32[7,16,8]{1,2,0:T(8,128)S(1)}, f32[7,16,8]{1,2,0:T(8,128)}, u32[]{:S(2)}) %copy-start.4) | copy-done | bytes 3608
  4.4 0.1 copy.21
  4.5 0.1 reshape.28
  4.6 0.1 fusion.5
  4.7 0.1 pad_slice_fusion
  4.7 0.1 concatenate.25
  4.8 0.1 concatenate.24
  4.9 3.0 %collective-permute-start = (f32[16,128]{1,0:T(8,128)S(1)}, f32[16,128]{1,0:T(8,128)S(1)}, u32[]{:S(2)}, u32[]{:S(2)}) collective-permute-start(f32[16,128]{1,0:T(8,128)S(1)} %get-tuple-element.19), channel_id=1, source_target_pairs={{0,8},{8,0},{16,24},{24,16},{1,9},{9,1},{17,25},{25,17},{2,10},{10... | collective-permute-start | bytes 24584 | tf_op jit(solution)/shard_map/ppermute | solution.py:124
  8.0 0.6 %collective-permute-start.1 = (f32[16,128]{1,0:T(8,128)S(1)}, f32[16,128]{1,0:T(8,128)S(1)}, u32[]{:S(2)}, u32[]{:S(2)}) collective-permute-start(f32[16,128]{1,0:T(8,128)S(1)} %get-tuple-element.18), channel_id=1, source_target_pairs={{8,16},{16,8},{9,17},{17,9},{10,18},{18,10},{11,19},{19,11},{12,20... | collective-permute-start | bytes 24584 | tf_op jit(solution)/shard_map/ppermute | solution.py:125
  8.6 1.0 %collective-permute-done = f32[16,128]{1,0:T(8,128)S(1)} collective-permute-done((f32[16,128]{1,0:T(8,128)S(1)}, f32[16,128]{1,0:T(8,128)S(1)}, u32[]{:S(2)}, u32[]{:S(2)}) %collective-permute-start) | collective-permute-done | bytes 8224 | tf_op jit(solution)/shard_map/ppermute | solution.py:124
  9.6 0.0 collective-permute-done.1
  9.6 2.2 %collective-permute-start.2 = (f32[72,128]{1,0:T(8,128)S(1)}, f32[72,128]{1,0:T(8,128)S(1)}, u32[]{:S(2)}, u32[]{:S(2)}) collective-permute-start(f32[72,128]{1,0:T(8,128)S(1)} %concatenate.26), channel_id=1, source_target_pairs={{0,2},{1,3},{2,0},{3,1},{4,6},{5,7},{6,4},{7,5},{8,10},{9,11},{10,... | collective-permute-start | bytes 110600 | tf_op jit(solution)/shard_map/ppermute | solution.py:116
  11.8 2.6 %collective-permute-start.3 = (f32[72,128]{1,0:T(8,128)S(1)}, f32[72,128]{1,0:T(8,128)S(1)}, u32[]{:S(2)}, u32[]{:S(2)}) collective-permute-start(f32[72,128]{1,0:T(8,128)S(1)} %concatenate.26), channel_id=1, source_target_pairs={{0,4},{1,5},{2,6},{3,7},{4,0},{5,1},{6,2},{7,3},{8,12},{9,13},{10,... | collective-permute-start | bytes 110600 | tf_op jit(solution)/shard_map/ppermute | solution.py:116
  14.4 0.0 collective-permute-start.4
  14.4 0.0 collective-permute-done.2
  14.4 3.0 %collective-permute-done.3 = f32[72,128]{1,0:T(8,128)S(1)} collective-permute-done((f32[72,128]{1,0:T(8,128)S(1)}, f32[72,128]{1,0:T(8,128)S(1)}, u32[]{:S(2)}, u32[]{:S(2)}) %collective-permute-start.3) | collective-permute-done | bytes 36896 | tf_op jit(solution)/shard_map/ppermute | solution.py:116
  17.4 2.8 %collective-permute-done.4 = f32[72,128]{1,0:T(8,128)S(1)} collective-permute-done((f32[72,128]{1,0:T(8,128)S(1)}, f32[72,128]{1,0:T(8,128)S(1)}, u32[]{:S(2)}, u32[]{:S(2)}) %collective-permute-start.4) | collective-permute-done | bytes 36896 | tf_op jit(solution)/shard_map/ppermute | solution.py:116
  20.1 0.1 collective-permute-start.5
  20.3 1.3 %collective-permute-done.5 = f32[4,72,128]{2,1,0:T(8,128)S(1)} collective-permute-done((f32[4,72,128]{2,1,0:T(8,128)S(1)}, f32[4,72,128]{2,1,0:T(8,128)S(1)}, u32[]{:S(2)}, u32[]{:S(2)}) %collective-permute-start.5) | collective-permute-done | bytes 147488 | tf_op jit(solution)/shard_map/ppermute | solution.py:116
  21.6 0.0 copy-start.1
  21.6 0.7 %copy-done.1 = f32[8,72,128]{2,1,0:T(8,128)} copy-done((f32[8,72,128]{2,1,0:T(8,128)}, f32[8,72,128]{2,1,0:T(8,128)S(1)}, u32[]{:S(2)}) %copy-start.1) | copy-done | bytes 294936
  22.3 2.3 %band.1 = (bf16[18,1024]{1,0:T(8,128)(2,1)}, f32[16,128]{1,0:T(8,128)}) custom-call(f32[8,72,128]{2,1,0:T(8,128)} %copy-done.1), custom_call_target="tpu_custom_call" | custom-call | tf_op jit(solution)/shard_map/band/pallas_call | solution.py:104
  24.6 0.0 copy-done
  24.6 1.0 %fusion = f32[18,4,128]{2,0,1:T(8,128)S(1)} fusion(bf16[1024,4,128]{2,1,0:T(4,128)(2,1)S(1)} %copy-done, bf16[18,1024]{1,0:T(8,128)(2,1)} %get-tuple-element.6), kind=kOutput, calls=%fused_computation | convolution fusion | flops 18874368 | bytes 1122304 | tf_op jit(solution)/shard_map/rc,cam->ram/dot_general | solution.py:172
  25.7 0.0 copy-start.5
  25.7 2.5 %collective-permute-start.8 = (f32[18,1,128]{2,0,1:T(8,128)S(1)}, f32[18,1,128]{2,0,1:T(8,128)S(1)}, u32[]{:S(2)}, u32[]{:S(2)}) collective-permute-start(f32[18,1,128]{2,0,1:T(8,128)S(1)} %get-tuple-element.16), channel_id=1, source_target_pairs={{0,24},{8,16},{16,8},{24,0},{1,25},{9,17},{17,9},{25,1},{2,26},{10... | collective-permute-start | bytes 27656 | tf_op jit(solution)/shard_map/ppermute | solution.py:116
  28.2 3.8 %collective-permute-start.7 = (f32[18,1,128]{2,0,1:T(8,128)S(1)}, f32[18,1,128]{2,0,1:T(8,128)S(1)}, u32[]{:S(2)}, u32[]{:S(2)}) collective-permute-start(f32[18,1,128]{2,0,1:T(8,128)S(1)} %get-tuple-element.17), channel_id=1, source_target_pairs={{0,16},{8,24},{16,0},{24,8},{1,17},{9,25},{17,1},{25,9},{2,18},{10... | collective-permute-start | bytes 27656 | tf_op jit(solution)/shard_map/ppermute | solution.py:116
  32.0 1.0 %collective-permute-start.6 = (f32[18,1,128]{2,0,1:T(8,128)S(1)}, f32[18,1,128]{2,0,1:T(8,128)S(1)}, u32[]{:S(2)}, u32[]{:S(2)}) collective-permute-start(f32[18,1,128]{2,0,1:T(8,128)S(1)} %get-tuple-element.15), channel_id=1, source_target_pairs={{0,8},{8,0},{16,24},{24,16},{1,9},{9,1},{17,25},{25,17},{2,10},{10... | collective-permute-start | bytes 27656 | tf_op jit(solution)/shard_map/ppermute | solution.py:116
  33.0 0.0 copy-done.5
  33.0 0.1 reshape.29
  33.1 0.7 %copy.23 = f32[2,8,16,8]{2,3,1,0:T(8,128)} copy(f32[2,8,16,8]{3,2,1,0:T(8,128)S(1)} %reshape.29) | data formatting | bytes 16384
  33.9 0.0 collective-permute-done.8
  33.9 0.0 collective-permute-done.7
  33.9 1.9 %collective-permute-done.6 = f32[18,1,128]{2,0,1:T(8,128)S(1)} collective-permute-done((f32[18,1,128]{2,0,1:T(8,128)S(1)}, f32[18,1,128]{2,0,1:T(8,128)S(1)}, u32[]{:S(2)}, u32[]{:S(2)}) %collective-permute-start.6) | collective-permute-done | bytes 9248 | tf_op jit(solution)/shard_map/ppermute | solution.py:116
  35.8 0.6 %slice.54 = f32[16,1,128]{2,0,1:T(8,128)} slice(f32[18,1,128]{2,0,1:T(8,128)S(1)} %add_add_fusion), slice={[0:16], [0:1], [0:128]} | slice | bytes 16384 | tf_op jit(solution)/shard_map/slice | solution.py:174
  36.4 0.6 %slice.55 = f32[2,1,128]{2,0,1:T(2,128)} slice(f32[18,1,128]{2,0,1:T(8,128)S(1)} %add_add_fusion), slice={[16:18], [0:1], [0:128]} | slice | bytes 2048 | tf_op jit(solution)/shard_map/slice | solution.py:175
  (16 shorter events, 0.1 us)
Async XLA Ops:
  0.6 24.0 %copy-start = (bf16[1024,4,128]{2,1,0:T(4,128)(2,1)S(1)}, bf16[1024,4,128]{2,1,0:T(4,128)(2,1)}, u32[]{:S(2)}) copy-start(bf16[1024,4,128]{2,1,0:T(4,128)(2,1)} %param.9) | copy-start | bytes 3145732
  1.9 0.8 %copy-start.2 = (f32[8,16,8]{1,2,0:T(8,128)S(1)}, f32[8,16,8]{1,2,0:T(8,128)}, u32[]{:S(2)}) copy-start(f32[8,16,8]{1,2,0:T(8,128)} %param.6) | copy-start | bytes 12292
  2.8 0.8 %copy-start.3 = (f32[8,16,8]{1,2,0:T(8,128)S(1)}, f32[8,16,8]{1,2,0:T(8,128)}, u32[]{:S(2)}) copy-start(f32[8,16,8]{1,2,0:T(8,128)} %param.7) | copy-start | bytes 12292
  3.6 0.8 %copy-start.4 = (f32[7,16,8]{1,2,0:T(8,128)S(1)}, f32[7,16,8]{1,2,0:T(8,128)}, u32[]{:S(2)}) copy-start(f32[7,16,8]{1,2,0:T(8,128)} %param.8) | copy-start | bytes 10756
  4.9 4.7 %collective-permute-start = (f32[16,128]{1,0:T(8,128)S(1)}, f32[16,128]{1,0:T(8,128)S(1)}, u32[]{:S(2)}, u32[]{:S(2)}) collective-permute-start(f32[16,128]{1,0:T(8,128)S(1)} %get-tuple-element.19), channel_id=1, source_target_pairs={{0,8},{8,0},{16,24},{24,16},{1,9},{9,1},{17,25},{25,17},{2,10},{10... | collective-permute-start | bytes 24584 | tf_op jit(solution)/shard_map/ppermute | solution.py:124
  8.0 1.6 %collective-permute-start.1 = (f32[16,128]{1,0:T(8,128)S(1)}, f32[16,128]{1,0:T(8,128)S(1)}, u32[]{:S(2)}, u32[]{:S(2)}) collective-permute-start(f32[16,128]{1,0:T(8,128)S(1)} %get-tuple-element.18), channel_id=1, source_target_pairs={{8,16},{16,8},{9,17},{17,9},{10,18},{18,10},{11,19},{19,11},{12,20... | collective-permute-start | bytes 24584 | tf_op jit(solution)/shard_map/ppermute | solution.py:125
  9.6 4.8 %collective-permute-start.2 = (f32[72,128]{1,0:T(8,128)S(1)}, f32[72,128]{1,0:T(8,128)S(1)}, u32[]{:S(2)}, u32[]{:S(2)}) collective-permute-start(f32[72,128]{1,0:T(8,128)S(1)} %concatenate.26), channel_id=1, source_target_pairs={{0,2},{1,3},{2,0},{3,1},{4,6},{5,7},{6,4},{7,5},{8,10},{9,11},{10,... | collective-permute-start | bytes 110600 | tf_op jit(solution)/shard_map/ppermute | solution.py:116
  11.8 5.6 %collective-permute-start.3 = (f32[72,128]{1,0:T(8,128)S(1)}, f32[72,128]{1,0:T(8,128)S(1)}, u32[]{:S(2)}, u32[]{:S(2)}) collective-permute-start(f32[72,128]{1,0:T(8,128)S(1)} %concatenate.26), channel_id=1, source_target_pairs={{0,4},{1,5},{2,6},{3,7},{4,0},{5,1},{6,2},{7,3},{8,12},{9,13},{10,... | collective-permute-start | bytes 110600 | tf_op jit(solution)/shard_map/ppermute | solution.py:116
  14.4 5.8 %collective-permute-start.4 = (f32[72,128]{1,0:T(8,128)S(1)}, f32[72,128]{1,0:T(8,128)S(1)}, u32[]{:S(2)}, u32[]{:S(2)}) collective-permute-start(f32[72,128]{1,0:T(8,128)S(1)} %concatenate.26), channel_id=1, source_target_pairs={{0,6},{1,7},{2,4},{3,5},{4,2},{5,3},{6,0},{7,1},{8,14},{9,15},{10,... | collective-permute-start | bytes 110600 | tf_op jit(solution)/shard_map/ppermute | solution.py:116
  20.1 1.4 %collective-permute-start.5 = (f32[4,72,128]{2,1,0:T(8,128)S(1)}, f32[4,72,128]{2,1,0:T(8,128)S(1)}, u32[]{:S(2)}, u32[]{:S(2)}) collective-permute-start(f32[4,72,128]{2,1,0:T(8,128)S(1)} %pad_maximum_fusion), channel_id=1, source_target_pairs={{0,1},{1,0},{2,3},{3,2},{4,5},{5,4},{6,7},{7,6},{8,9},{9,8},{10,11... | collective-permute-start | bytes 442376 | tf_op jit(solution)/shard_map/ppermute | solution.py:116
  21.6 0.7 %copy-start.1 = (f32[8,72,128]{2,1,0:T(8,128)}, f32[8,72,128]{2,1,0:T(8,128)S(1)}, u32[]{:S(2)}) copy-start(f32[8,72,128]{2,1,0:T(8,128)S(1)} %constant_dynamic-update-slice_fusion.band_ref) | copy-start | bytes 884740
  25.7 7.3 %copy-start.5 = (f32[16,128]{1,0:T(8,128)S(1)}, f32[16,128]{1,0:T(8,128)}, u32[]{:S(2)}) copy-start(f32[16,128]{1,0:T(8,128)} %get-tuple-element.5) | copy-start | bytes 24580
  25.7 8.2 %collective-permute-start.8 = (f32[18,1,128]{2,0,1:T(8,128)S(1)}, f32[18,1,128]{2,0,1:T(8,128)S(1)}, u32[]{:S(2)}, u32[]{:S(2)}) collective-permute-start(f32[18,1,128]{2,0,1:T(8,128)S(1)} %get-tuple-element.16), channel_id=1, source_target_pairs={{0,24},{8,16},{16,8},{24,0},{1,25},{9,17},{17,9},{25,1},{2,26},{10... | collective-permute-start | bytes 27656 | tf_op jit(solution)/shard_map/ppermute | solution.py:116
  28.2 5.6 %collective-permute-start.7 = (f32[18,1,128]{2,0,1:T(8,128)S(1)}, f32[18,1,128]{2,0,1:T(8,128)S(1)}, u32[]{:S(2)}, u32[]{:S(2)}) collective-permute-start(f32[18,1,128]{2,0,1:T(8,128)S(1)} %get-tuple-element.17), channel_id=1, source_target_pairs={{0,16},{8,24},{16,0},{24,8},{1,17},{9,25},{17,1},{25,9},{2,18},{10... | collective-permute-start | bytes 27656 | tf_op jit(solution)/shard_map/ppermute | solution.py:116
  32.0 3.7 %collective-permute-start.6 = (f32[18,1,128]{2,0,1:T(8,128)S(1)}, f32[18,1,128]{2,0,1:T(8,128)S(1)}, u32[]{:S(2)}, u32[]{:S(2)}) collective-permute-start(f32[18,1,128]{2,0,1:T(8,128)S(1)} %get-tuple-element.15), channel_id=1, source_target_pairs={{0,8},{8,0},{16,24},{24,16},{1,9},{9,1},{17,25},{25,17},{2,10},{10... | collective-permute-start | bytes 27656 | tf_op jit(solution)/shard_map/ppermute | solution.py:116

commit v2 on v1

--- a/solution.py
+++ b/solution.py
@@ -6,7 +6,9 @@
 from jax.experimental.pallas import tpu as pltpu
 from jax.sharding import PartitionSpec as P
 
+
 DIRECT = 4
+GRANT = 4 << 20
 
 
 def roll(value, shift, axis=-1):
@@ -14,26 +16,100 @@
     return pltpu.roll(value, shift % value.shape[axis], axis)
 
 
-def band_kernel(rows, cols, blocks, exchanged, band_ref, vec_ref, adjoint_ref, all_ref):
+def pack_kernel(rows, cols, forcing_hbm, zonal_hbm, merid_hbm, mixing_hbm, main_ref, near_ref, far_ref,
+                forcing_ref, zonal_ref, merid_ref, mixing_ref, sems):
+    copies = [
+        pltpu.make_async_copy(source, target, sems.at[i])
+        for i, (source, target) in enumerate(
+            ((forcing_hbm, forcing_ref), (zonal_hbm, zonal_ref), (merid_hbm, merid_ref), (mixing_hbm, mixing_ref)))
+    ]
+    for copy in copies:
+        copy.start()
+    cells = rows * cols
+    two = 2 * cols
+    lane = lax.broadcasted_iota(jnp.int32, (2, 8, cells), 2)
+    level = lax.broadcasted_iota(jnp.int32, (2, 8, cells), 1)
+    half = lax.broadcasted_iota(jnp.int32, (2, 8, cells), 0)
+    group = lane // cols
+    plane = half * 8 + level
+
+    def flat(planes):
+        value = planes.reshape(16 * cols, rows).T.reshape(2, 8, cells)
+        for step in (1, 2, 4):
+            upper = roll(roll(value, -step, 1), step * cols)
+            lower = roll(roll(value, step, 1), -step * cols)
+            here, there = (plane // step) % 2, (group // step) % 2
+            value = jnp.where(here == there, value, jnp.where(here == 0, upper, lower))
+        crossed = jnp.concatenate([value[1:], value[:1]], 0)
+        crossed = roll(crossed, 8 * cols)
+        return jnp.where(half == group // 8, value, crossed)
+
+    copies[0].wait()
+    forced = flat(forcing_ref[1].reshape(16, cols, rows))
+    first = flat(forcing_ref[0].reshape(16, cols, rows))
+    copies[1].wait()
+    copies[3].wait()
+    pair = flat(jnp.concatenate([zonal_ref[...], mixing_ref[...], jnp.zeros((1, cols, rows), jnp.float32)], 0))
+    copies[2].wait()
+    merid = merid_ref[...]
+    lone = flat(jnp.concatenate([merid, jnp.zeros_like(merid)], 0))
+    place = lax.axis_index("lat")
+    top = jnp.where(place == lax.axis_size("lat") - 1, 1, 0)
+    lone = jnp.where((group == rows - 1) & (top == 1), 0.0, lone)
+    main_ref[0:16] = forced.reshape(16, cells)
+    main_ref[16:32] = first.reshape(16, cells)
+    main_ref[32:48] = pair.reshape(16, cells)
+    main_ref[48:56] = lone[0]
+    upper = jnp.zeros((2, 8, cells), jnp.float32)
+    lower = jnp.zeros((2, 8, cells), jnp.float32)
+    for i, value in enumerate((forced, first, pair, lone)):
+        start = 2 * two * i
+        lower = jnp.where((lane >= start) & (lane < start + two), roll(value, start), lower)
+        upper = jnp.where((lane >= start + two) & (lane < start + 2 * two), roll(value, start + 2 * two), upper)
+    even = jnp.where(place % 2 == 0, 1, 0)
+    mine = jnp.broadcast_to(even, upper.shape) == 1
+    near_ref[...] = jnp.where(mine, upper, lower).reshape(16, cells)
+    far_ref[...] = jnp.where(mine, lower, upper).reshape(16, cells)
+
+
+def packed_fields(forcing, zonal, meridional, mixing):
+    _, rows, cols = zonal.shape
+    cells = rows * cols
+    fields = (forcing, zonal, meridional, mixing)
+    values = [pltpu.with_memory_space_constraint(jnp.swapaxes(v, -1, -2), pltpu.HBM) for v in fields]
+    edge = jax.ShapeDtypeStruct((16, cells), jnp.float32)
+    return pl.pallas_call(
+        functools.partial(pack_kernel, rows, cols),
+        out_shape=(jax.ShapeDtypeStruct((56, cells), jnp.float32), edge, edge),
+        in_specs=[pl.BlockSpec(memory_space=pltpu.HBM)] * 4,
+        out_specs=[pl.BlockSpec(memory_space=pltpu.VMEM)] * 3,
+        scratch_shapes=[pltpu.VMEM(v.shape, jnp.float32) for v in values] + [pltpu.SemaphoreType.DMA((4,))],
+        compiler_params=pltpu.CompilerParams(vmem_limit_bytes=GRANT),
+        name="pack",
+    )(*values)
+
+
+def band_kernel(rows, cols, blocks, exchanged, *refs):
+    *band_refs, vec_ref, adjoint_ref, all_ref = refs
     me = lax.axis_index("lon")
     cells = rows * cols
     two = 2 * cols
-
-    def load(block):
-        if exchanged:
-            apart = jnp.bitwise_xor(block, me)
-            place = (apart % 2) * (blocks // 2) + apart // 2
-        else:
-            place = block
-        return band_ref[place]
-
-    loaded = [load(block) for block in range(blocks)]
+    if exchanged:
+        same, other = band_refs
+        odd = jnp.broadcast_to(me % 2, (72, cells)) == 1
+        loaded = []
+        for chip in range(blocks // 2):
+            place = jnp.bitwise_xor(chip, me // 2)
+            here, there = same[place], other[place]
+            loaded += [jnp.where(odd, there, here), jnp.where(odd, here, there)]
+    else:
+        loaded = [band_refs[0][block] for block in range(blocks)]
 
     def field(start, count):
         return jnp.stack([block[start : start + 8 * count].reshape(count, 8, cells) for block in loaded])
 
     forced, first, zonal, merid, mixing, halo = (
-        field(0, 2), field(16, 2), field(32, 1), field(40, 1), field(48, 1), field(56, 2))
+        field(0, 2), field(16, 2), field(32, 1), field(48, 1), field(40, 1), field(56, 2))
     lane = lax.broadcasted_iota(jnp.int32, (1, 1, 8, cells), 3)
     column = lane % cols
 
@@ -104,11 +180,12 @@
     return pl.pallas_call(
         functools.partial(band_kernel, rows, cols, blocks, exchanged),
         out_shape=(jax.ShapeDtypeStruct((18, blocks * cells), jnp.bfloat16), jax.ShapeDtypeStruct((16, cells), jnp.float32)),
-        in_specs=[pl.BlockSpec(memory_space=pltpu.VMEM)],
+        in_specs=[pl.BlockSpec(memory_space=pltpu.VMEM)] * len(band),
         out_specs=(pl.BlockSpec(memory_space=pltpu.VMEM), pl.BlockSpec(memory_space=pltpu.VMEM)),
         scratch_shapes=[pltpu.VMEM((blocks, 16, cells), jnp.float32)],
+        compiler_params=pltpu.CompilerParams(vmem_limit_bytes=GRANT * (1 if exchanged else 4)),
         name="band",
-    )(band)
+    )(*band)
 
 
 def swapped(value, axis, apart):
@@ -116,23 +193,23 @@
     return lax.ppermute(value, axis, [(i, i ^ apart) for i in range(peers) if i ^ apart < peers])
 
 
-def along_lat(upper, lower):
+def along_lat(nearer, farther):
     peers = lax.axis_size("lat")
-    even = lax.axis_index("lat") % 2 == 0
-    pairs = [(i, i ^ 1) for i in range(peers)]
     others = [(i, i + 1 if i % 2 else i - 1) for i in range(1, peers - 1)]
-    nearer = lax.ppermute(jnp.where(even, upper, lower), "lat", pairs)
-    farther = lax.ppermute(jnp.where(even, lower, upper), "lat", others)
+    farther = lax.ppermute(farther, "lat", others)
+    nearer = swapped(nearer, "lat", 1)
     return nearer + farther
 
 
 def gathered(packed):
     peers = lax.axis_size("lon")
     if peers > 2 * DIRECT:
-        return lax.all_gather(packed, "lon", axis=0), False
-    pieces = [packed] + [swapped(packed, "lon", apart) for apart in range(2, peers, 2)]
-    own = jnp.stack(pieces)
-    return jnp.concatenate([own, swapped(own, "lon", 1)], 0), True
+        return (lax.all_gather(packed, "lon", axis=0),), False
+    pieces = [packed]
+    for apart in range(2, peers, 2):
+        pieces.append(swapped(packed, "lon", apart))
+    same = jnp.stack(pieces)
+    return (same, swapped(same, "lon", 1)), True
 
 
 def scattered(total):
@@ -149,24 +226,8 @@
 
 def shards(forcing, zonal, meridional, mixing, panel):
     levels, rows, cols = zonal.shape
-    cells = rows * cols
-    row_index = lax.axis_index("lat") * rows + jnp.arange(rows, dtype=jnp.int32)
-    below_top = row_index < rows * lax.axis_size("lat") - 1
-    masked = jnp.where(below_top[None, :, None], meridional, 0.0)
-    forced = forcing[1].reshape(2 * levels, cells)
-    first = forcing[0].reshape(2 * levels, cells)
-    across = zonal.reshape(levels, cells)
-    along = masked.reshape(levels, cells)
-    mixed = jnp.concatenate([mixing.reshape(levels - 1, cells), jnp.zeros((1, cells), jnp.float32)], 0)
-    pair = jnp.concatenate([across, mixed], 0)
-    lone = jnp.concatenate([along, jnp.zeros_like(along)], 0)
-    two = 2 * cols
-    blank = jnp.zeros((2 * levels, two), jnp.float32)
-    sources = (forced, first, pair, lone)
-    upper = jnp.concatenate([piece for s in sources for piece in (blank, s[:, cells - two :])], 1)
-    lower = jnp.concatenate([piece for s in sources for piece in (s[:, :two], blank)], 1)
-    halo = along_lat(upper, lower)
-    packed = jnp.concatenate([forced, first, across, along, mixed, halo], 0)
+    main, nearer, farther = packed_fields(forcing, zonal, meridional, mixing)
+    packed = jnp.concatenate([main, along_lat(nearer, farther)], 0)
     band, exchanged = gathered(packed)
     vectors, adjoint = band_vectors(band, rows, cols, lax.axis_size("lon"), exchanged)
     total = jnp.einsum("rc,cam->ram", vectors, panel, preferred_element_type=jnp.float32)

time: 37.4 us -> 32.3 us (0.86)
  local copies, waits for them, and re-layouts: 6.91 us -> 2.01 us
  matrix products: 1.05 us -> 0.25 us
  Pallas kernels: 2.34 us -> 2.9 us
  waiting for transfers between devices: 9.89 us -> 10.4 us
    ppermute x7 -> x8, starting transfers between devices: 12.1 us -> 15.2 us  [swapped(): lax.ppermute(value, axis, [(i, i ^ apart) for i in range(peers) if i ^ ap...]
    ppermute x2 -> x1, starting transfers between devices: 3.68 us -> 0.65 us  [along_lat(): farther = lax.ppermute(farther, 'lat', others)]
    unnamed x19 -> x3, local copies, waits for them, and re-layouts: 3.56 us -> 0.74 us
    pallas_call x0 -> x1, Pallas kernels: none -> 2.17 us  [packed_fields(): pl.pallas_call(functools.partial(pack_kernel, rows, cols), out_shape=(jax...]
    pallas_call x1, Pallas kernels: 2.34 us -> 0.73 us  [band_vectors(): pl.pallas_call(functools.partial(band_kernel, rows, cols, blocks, exchang...]
    ppermute x7 -> x8, waiting for transfers between devices: 8.93 us -> 10.4 us  [swapped(): lax.ppermute(value, axis, [(i, i ^ apart) for i in range(peers) if i ^ ap...]
    slice x5 -> x0, local copies, waits for them, and re-layouts: 1.29 us -> none  [the longest x2 1.06 us: shards(): first = forcing[0].reshape(2 * levels, cells)]
    ppermute x2 -> x1, waiting for transfers between devices: 0.96 us -> 0.01 us  [along_lat(): farther = lax.ppermute(farther, 'lat', others)]
  transfers between devices with their start and end apart: 9 -> 9, of which waited for: 5 -> 6; matrix products, arithmetic and copies ran while one was open for 2% -> 3% of each run, Pallas kernels for 0% -> 0%
where the time goes in v2:
time: 32.3 us; the launch traced here: 32.2 us
  starting transfers between devices  15.8 us (49%)
  waiting for transfers between devices  10.4 us (32%)
  Pallas kernels  2.9 us (9%)
  local copies, waits for them, and re-layouts  2.01 us (6%)
  between operations  0.73 us (2%)
    ppermute x8, starting transfers between devices, swapped(): lax.ppermute(value, axis, [(i, i ^ apart) for i in range(peers) if i ^ ap...  15.2 us
    ppermute x8, waiting for transfers between devices, swapped(): lax.ppermute(value, axis, [(i, i ^ apart) for i in range(peers) if i ^ ap...  10.4 us
    pallas_call x1, Pallas kernels, packed_fields(): pl.pallas_call(functools.partial(pack_kernel, rows, cols), out_shape=(jax...  2.17 us
    unnamed x3, local copies, waits for them, and re-layouts  0.74 us
    pallas_call x1, Pallas kernels, band_vectors(): pl.pallas_call(functools.partial(band_kernel, rows, cols, blocks, exchang...  0.73 us
    ppermute x1, starting transfers between devices, along_lat(): farther = lax.ppermute(farther, 'lat', others)  0.65 us
  transfers between devices with their start and end apart: 9, of which 6 were waited for; matrix products, arithmetic and copies ran while one was open for 3% of the time, Pallas kernels for 0%

profile of v2, /device:TPU:0, one launch (start us, length us, event | category | flops | bytes accessed | tf_op | source)
XLA Modules:
  0.0 32.2 jit_solution(8763397945750061423)
XLA Ops:
  0.6 0.0 copy-start
  0.6 2.2 %pack.1 = (f32[56,128]{1,0:T(8,128)S(1)}, f32[16,128]{1,0:T(8,128)S(1)}, f32[16,128]{1,0:T(8,128)S(1)}) custom-call(f32[2,2,8,8,16]{4,3,2,1,0:T(8,128)} %bitcast.16, f32[8,8,16]{2,1,0:T(8,128)} %bitcast.20, f32[8,8,16]{2,1,0:T(8,128)} %bitcast.21, f32[7,8,16]{2,1,0:T(8,128)} %bitcast.22), custom_call_target="tpu_custom_call" | custom-call | tf_op jit(solution)/shard_map/pack/pallas_call | solution.py:81
  2.8 3.0 %collective-permute-start = (f32[16,128]{1,0:T(8,128)S(1)}, f32[16,128]{1,0:T(8,128)S(1)}, u32[]{:S(2)}, u32[]{:S(2)}) collective-permute-start(f32[16,128]{1,0:T(8,128)S(1)} %get-tuple-element.9), channel_id=1, source_target_pairs={{0,8},{8,0},{16,24},{24,16},{1,9},{9,1},{17,25},{25,17},{2,10},{10... | collective-permute-start | bytes 24584 | tf_op jit(solution)/shard_map/ppermute | solution.py:193
  5.9 0.6 %collective-permute-start.1 = (f32[16,128]{1,0:T(8,128)S(1)}, f32[16,128]{1,0:T(8,128)S(1)}, u32[]{:S(2)}, u32[]{:S(2)}) collective-permute-start(f32[16,128]{1,0:T(8,128)S(1)} %get-tuple-element.10), channel_id=1, source_target_pairs={{8,16},{16,8},{9,17},{17,9},{10,18},{18,10},{11,19},{19,11},{12,20... | collective-permute-start | bytes 24584 | tf_op jit(solution)/shard_map/ppermute | solution.py:199
  6.5 1.0 %collective-permute-done = f32[16,128]{1,0:T(8,128)S(1)} collective-permute-done((f32[16,128]{1,0:T(8,128)S(1)}, f32[16,128]{1,0:T(8,128)S(1)}, u32[]{:S(2)}, u32[]{:S(2)}) %collective-permute-start) | collective-permute-done | bytes 8224 | tf_op jit(solution)/shard_map/ppermute | solution.py:193
  7.5 0.0 collective-permute-done.1
  7.5 2.2 %collective-permute-start.2 = (f32[72,128]{1,0:T(8,128)S(1)}, f32[72,128]{1,0:T(8,128)S(1)}, u32[]{:S(2)}, u32[]{:S(2)}) collective-permute-start(f32[72,128]{1,0:T(8,128)S(1)} %get-tuple-element.23), channel_id=1, source_target_pairs={{0,2},{1,3},{2,0},{3,1},{4,6},{5,7},{6,4},{7,5},{8,10},{9,11},{10,... | collective-permute-start | bytes 110600 | tf_op jit(solution)/shard_map/ppermute | solution.py:193
  9.7 2.6 %collective-permute-start.3 = (f32[72,128]{1,0:T(8,128)S(1)}, f32[72,128]{1,0:T(8,128)S(1)}, u32[]{:S(2)}, u32[]{:S(2)}) collective-permute-start(f32[72,128]{1,0:T(8,128)S(1)} %get-tuple-element.23), channel_id=1, source_target_pairs={{0,4},{1,5},{2,6},{3,7},{4,0},{5,1},{6,2},{7,3},{8,12},{9,13},{10,... | collective-permute-start | bytes 110600 | tf_op jit(solution)/shard_map/ppermute | solution.py:193
  12.3 0.0 collective-permute-start.4
  12.3 0.0 collective-permute-done.2
  12.3 3.0 %collective-permute-done.3 = f32[72,128]{1,0:T(8,128)S(1)} collective-permute-done((f32[72,128]{1,0:T(8,128)S(1)}, f32[72,128]{1,0:T(8,128)S(1)}, u32[]{:S(2)}, u32[]{:S(2)}) %collective-permute-start.3) | collective-permute-done | bytes 36896 | tf_op jit(solution)/shard_map/ppermute | solution.py:193
  15.3 2.8 %collective-permute-done.4 = f32[72,128]{1,0:T(8,128)S(1)} collective-permute-done((f32[72,128]{1,0:T(8,128)S(1)}, f32[72,128]{1,0:T(8,128)S(1)}, u32[]{:S(2)}, u32[]{:S(2)}) %collective-permute-start.4) | collective-permute-done | bytes 36896 | tf_op jit(solution)/shard_map/ppermute | solution.py:193
  18.0 0.1 collective-permute-start.5
  18.1 1.3 %collective-permute-done.5.refs_1_ = f32[4,72,128]{2,1,0:T(8,128)S(1)} collective-permute-done((f32[4,72,128]{2,1,0:T(8,128)S(1)}, f32[4,72,128]{2,1,0:T(8,128)S(1)}, u32[]{:S(2)}, u32[]{:S(2)}) %collective-permute-start.5) | collective-permute-done | bytes 147488 | tf_op jit(solution)/shard_map/ppermute | solution.py:193
  19.5 0.7 %band.1 = (bf16[18,1024]{1,0:T(8,128)(2,1)S(1)}, f32[16,128]{1,0:T(8,128)S(1)}) custom-call(f32[4,72,128]{2,1,0:T(8,128)S(1)} %pad_maximum_fusion.refs_0_, f32[4,72,128]{2,1,0:T(8,128)S(1)} %collective-permute-done.5.refs_1_), custom_call_target="tpu_custom_call" | custom-call | tf_op jit(solution)/shard_map/band/pallas_call | solution.py:180
  20.2 0.0 copy-done
  20.2 0.3 fusion
  20.5 4.9 %collective-permute-start.6 = (f32[18,1,128]{2,0,1:T(8,128)S(1)}, f32[18,1,128]{2,0,1:T(8,128)S(1)}, u32[]{:S(2)}, u32[]{:S(2)}) collective-permute-start(f32[18,1,128]{2,0,1:T(8,128)S(1)} %get-tuple-element.19), channel_id=1, source_target_pairs={{0,8},{8,0},{16,24},{24,16},{1,9},{9,1},{17,25},{25,17},{2,10},{10... | collective-permute-start | bytes 27656 | tf_op jit(solution)/shard_map/ppermute | solution.py:193
  25.4 1.1 %collective-permute-start.7 = (f32[18,1,128]{2,0,1:T(8,128)S(1)}, f32[18,1,128]{2,0,1:T(8,128)S(1)}, u32[]{:S(2)}, u32[]{:S(2)}) collective-permute-start(f32[18,1,128]{2,0,1:T(8,128)S(1)} %get-tuple-element.21), channel_id=1, source_target_pairs={{0,16},{8,24},{16,0},{24,8},{1,17},{9,25},{17,1},{25,9},{2,18},{10... | collective-permute-start | bytes 27656 | tf_op jit(solution)/shard_map/ppermute | solution.py:193
  26.4 1.4 %collective-permute-start.8 = (f32[18,1,128]{2,0,1:T(8,128)S(1)}, f32[18,1,128]{2,0,1:T(8,128)S(1)}, u32[]{:S(2)}, u32[]{:S(2)}) collective-permute-start(f32[18,1,128]{2,0,1:T(8,128)S(1)} %get-tuple-element.20), channel_id=1, source_target_pairs={{0,24},{8,16},{16,8},{24,0},{1,25},{9,17},{17,9},{25,1},{2,26},{10... | collective-permute-start | bytes 27656 | tf_op jit(solution)/shard_map/ppermute | solution.py:193
  27.8 0.1 reshape.12
  27.9 0.7 %copy.13 = f32[2,8,16,8]{2,3,1,0:T(8,128)} copy(f32[2,8,16,8]{3,2,1,0:T(8,128)S(1)} %reshape.12) | data formatting | bytes 16384
  28.6 0.0 collective-permute-done.6
  28.6 0.4 %collective-permute-done.7 = f32[18,1,128]{2,0,1:T(8,128)S(1)} collective-permute-done((f32[18,1,128]{2,0,1:T(8,128)S(1)}, f32[18,1,128]{2,0,1:T(8,128)S(1)}, u32[]{:S(2)}, u32[]{:S(2)}) %collective-permute-start.7) | collective-permute-done | bytes 9248 | tf_op jit(solution)/shard_map/ppermute | solution.py:193
  29.1 2.0 %collective-permute-done.8 = f32[18,1,128]{2,0,1:T(8,128)S(1)} collective-permute-done((f32[18,1,128]{2,0,1:T(8,128)S(1)}, f32[18,1,128]{2,0,1:T(8,128)S(1)}, u32[]{:S(2)}, u32[]{:S(2)}) %collective-permute-start.8) | collective-permute-done | bytes 9248 | tf_op jit(solution)/shard_map/ppermute | solution.py:193
  31.0 0.6 %slice.8 = f32[16,1,128]{2,0,1:T(8,128)} slice(f32[18,1,128]{2,0,1:T(8,128)S(1)} %add_add_fusion), slice={[0:16], [0:1], [0:128]} | slice | bytes 16384 | tf_op jit(solution)/shard_map/slice | solution.py:235
  31.6 0.6 %slice.9 = f32[2,1,128]{2,0,1:T(2,128)} slice(f32[18,1,128]{2,0,1:T(8,128)S(1)} %add_add_fusion), slice={[16:18], [0:1], [0:128]} | slice | bytes 2048 | tf_op jit(solution)/shard_map/slice | solution.py:236
  (5 shorter events, 0.0 us)
Async XLA Ops:
  0.6 19.6 %copy-start = (bf16[1024,4,128]{2,1,0:T(4,128)(2,1)S(1)}, bf16[1024,4,128]{2,1,0:T(4,128)(2,1)}, u32[]{:S(2)}) copy-start(bf16[1024,4,128]{2,1,0:T(4,128)(2,1)} %param.9) | copy-start | bytes 3145732
  2.8 4.7 %collective-permute-start = (f32[16,128]{1,0:T(8,128)S(1)}, f32[16,128]{1,0:T(8,128)S(1)}, u32[]{:S(2)}, u32[]{:S(2)}) collective-permute-start(f32[16,128]{1,0:T(8,128)S(1)} %get-tuple-element.9), channel_id=1, source_target_pairs={{0,8},{8,0},{16,24},{24,16},{1,9},{9,1},{17,25},{25,17},{2,10},{10... | collective-permute-start | bytes 24584 | tf_op jit(solution)/shard_map/ppermute | solution.py:193
  5.9 1.6 %collective-permute-start.1 = (f32[16,128]{1,0:T(8,128)S(1)}, f32[16,128]{1,0:T(8,128)S(1)}, u32[]{:S(2)}, u32[]{:S(2)}) collective-permute-start(f32[16,128]{1,0:T(8,128)S(1)} %get-tuple-element.10), channel_id=1, source_target_pairs={{8,16},{16,8},{9,17},{17,9},{10,18},{18,10},{11,19},{19,11},{12,20... | collective-permute-start | bytes 24584 | tf_op jit(solution)/shard_map/ppermute | solution.py:199
  7.5 4.8 %collective-permute-start.2 = (f32[72,128]{1,0:T(8,128)S(1)}, f32[72,128]{1,0:T(8,128)S(1)}, u32[]{:S(2)}, u32[]{:S(2)}) collective-permute-start(f32[72,128]{1,0:T(8,128)S(1)} %get-tuple-element.23), channel_id=1, source_target_pairs={{0,2},{1,3},{2,0},{3,1},{4,6},{5,7},{6,4},{7,5},{8,10},{9,11},{10,... | collective-permute-start | bytes 110600 | tf_op jit(solution)/shard_map/ppermute | solution.py:193
  9.7 5.6 %collective-permute-start.3 = (f32[72,128]{1,0:T(8,128)S(1)}, f32[72,128]{1,0:T(8,128)S(1)}, u32[]{:S(2)}, u32[]{:S(2)}) collective-permute-start(f32[72,128]{1,0:T(8,128)S(1)} %get-tuple-element.23), channel_id=1, source_target_pairs={{0,4},{1,5},{2,6},{3,7},{4,0},{5,1},{6,2},{7,3},{8,12},{9,13},{10,... | collective-permute-start | bytes 110600 | tf_op jit(solution)/shard_map/ppermute | solution.py:193
  12.3 5.8 %collective-permute-start.4 = (f32[72,128]{1,0:T(8,128)S(1)}, f32[72,128]{1,0:T(8,128)S(1)}, u32[]{:S(2)}, u32[]{:S(2)}) collective-permute-start(f32[72,128]{1,0:T(8,128)S(1)} %get-tuple-element.23), channel_id=1, source_target_pairs={{0,6},{1,7},{2,4},{3,5},{4,2},{5,3},{6,0},{7,1},{8,14},{9,15},{10,... | collective-permute-start | bytes 110600 | tf_op jit(solution)/shard_map/ppermute | solution.py:193
  18.0 1.4 %collective-permute-start.5 = (f32[4,72,128]{2,1,0:T(8,128)S(1)}, f32[4,72,128]{2,1,0:T(8,128)S(1)}, u32[]{:S(2)}, u32[]{:S(2)}) collective-permute-start(f32[4,72,128]{2,1,0:T(8,128)S(1)} %pad_maximum_fusion.refs_0_), channel_id=1, source_target_pairs={{0,1},{1,0},{2,3},{3,2},{4,5},{5,4},{6,7},{7,6},{8,9},{9,8},{10,11... | collective-permute-start | bytes 442376 | tf_op jit(solution)/shard_map/ppermute | solution.py:193
  20.5 8.2 %collective-permute-start.6 = (f32[18,1,128]{2,0,1:T(8,128)S(1)}, f32[18,1,128]{2,0,1:T(8,128)S(1)}, u32[]{:S(2)}, u32[]{:S(2)}) collective-permute-start(f32[18,1,128]{2,0,1:T(8,128)S(1)} %get-tuple-element.19), channel_id=1, source_target_pairs={{0,8},{8,0},{16,24},{24,16},{1,9},{9,1},{17,25},{25,17},{2,10},{10... | collective-permute-start | bytes 27656 | tf_op jit(solution)/shard_map/ppermute | solution.py:193
  25.4 3.7 %collective-permute-start.7 = (f32[18,1,128]{2,0,1:T(8,128)S(1)}, f32[18,1,128]{2,0,1:T(8,128)S(1)}, u32[]{:S(2)}, u32[]{:S(2)}) collective-permute-start(f32[18,1,128]{2,0,1:T(8,128)S(1)} %get-tuple-element.21), channel_id=1, source_target_pairs={{0,16},{8,24},{16,0},{24,8},{1,17},{9,25},{17,1},{25,9},{2,18},{10... | collective-permute-start | bytes 27656 | tf_op jit(solution)/shard_map/ppermute | solution.py:193
  26.4 4.6 %collective-permute-start.8 = (f32[18,1,128]{2,0,1:T(8,128)S(1)}, f32[18,1,128]{2,0,1:T(8,128)S(1)}, u32[]{:S(2)}, u32[]{:S(2)}) collective-permute-start(f32[18,1,128]{2,0,1:T(8,128)S(1)} %get-tuple-element.20), channel_id=1, source_target_pairs={{0,24},{8,16},{16,8},{24,0},{1,25},{9,17},{17,9},{25,1},{2,26},{10... | collective-permute-start | bytes 27656 | tf_op jit(solution)/shard_map/ppermute | solution.py:193

commit v3 on v2

--- a/solution.py
+++ b/solution.py
@@ -9,6 +9,8 @@
 
 DIRECT = 4
 GRANT = 4 << 20
+EDGE_CROSS = 1
+CHIP_CROSS = 1
 
 
 def roll(value, shift, axis=-1):
@@ -66,10 +68,10 @@
         start = 2 * two * i
         lower = jnp.where((lane >= start) & (lane < start + two), roll(value, start), lower)
         upper = jnp.where((lane >= start + two) & (lane < start + 2 * two), roll(value, start + 2 * two), upper)
-    even = jnp.where(place % 2 == 0, 1, 0)
-    mine = jnp.broadcast_to(even, upper.shape) == 1
-    near_ref[...] = jnp.where(mine, upper, lower).reshape(16, cells)
-    far_ref[...] = jnp.where(mine, lower, upper).reshape(16, cells)
+    even = place % 2 == 0
+    near_ref[...] = jnp.where(even, upper, lower).reshape(16, cells)
+    ended = (place == 0) | ((place == lax.axis_size("lat") - 1) & ~even)
+    far_ref[...] = jnp.where(ended, 0.0, jnp.where(even, lower, upper)).reshape(16, cells)
 
 
 def packed_fields(forcing, zonal, meridional, mixing):
@@ -94,22 +96,25 @@
     me = lax.axis_index("lon")
     cells = rows * cols
     two = 2 * cols
+    mains, halos = [], []
     if exchanged:
         same, other = band_refs
-        odd = jnp.broadcast_to(me % 2, (72, cells)) == 1
-        loaded = []
         for chip in range(blocks // 2):
             place = jnp.bitwise_xor(chip, me // 2)
+            turned = (me + CHIP_CROSS * jnp.where(place == 0, 0, 1)) % 2 == 1
             here, there = same[place], other[place]
-            loaded += [jnp.where(odd, there, here), jnp.where(odd, here, there)]
+            pair = [jnp.where(turned, there, here), jnp.where(turned, here, there)]
+            mains += [piece[:56] for piece in pair]
+            halos += [piece[56:] for piece in (pair[::-1] if EDGE_CROSS else pair)]
     else:
-        loaded = [band_refs[0][block] for block in range(blocks)]
+        mains = [band_refs[0][block, :56] for block in range(blocks)]
+        halos = [band_refs[0][block ^ EDGE_CROSS, 56:] for block in range(blocks)]
 
     def field(start, count):
-        return jnp.stack([block[start : start + 8 * count].reshape(count, 8, cells) for block in loaded])
-
-    forced, first, zonal, merid, mixing, halo = (
-        field(0, 2), field(16, 2), field(32, 1), field(48, 1), field(40, 1), field(56, 2))
+        return jnp.stack([block[start : start + 8 * count].reshape(count, 8, cells) for block in mains])
+
+    forced, first, zonal, merid, mixing = field(0, 2), field(16, 2), field(32, 1), field(48, 1), field(40, 1)
+    halo = jnp.stack([block.reshape(2, 8, cells) for block in halos])
     lane = lax.broadcasted_iota(jnp.int32, (1, 1, 8, cells), 3)
     column = lane % cols
 
@@ -188,16 +193,19 @@
     )(*band)
 
 
-def swapped(value, axis, apart):
-    peers = lax.axis_size(axis)
-    return lax.ppermute(value, axis, [(i, i ^ apart) for i in range(peers) if i ^ apart < peers])
+def moved(value, target):
+    lats, lons = lax.axis_size("lat"), lax.axis_size("lon")
+    pairs = []
+    for lat in range(lats):
+        for lon in range(lons):
+            to_lat, to_lon = target(lat, lon)
+            pairs.append((lat * lons + lon, to_lat % lats * lons + to_lon))
+    return lax.ppermute(value, ("lat", "lon"), pairs)
 
 
 def along_lat(nearer, farther):
-    peers = lax.axis_size("lat")
-    others = [(i, i + 1 if i % 2 else i - 1) for i in range(1, peers - 1)]
-    farther = lax.ppermute(farther, "lat", others)
-    nearer = swapped(nearer, "lat", 1)
+    farther = moved(farther, lambda lat, lon: (lat + 1 if lat % 2 else lat - 1, lon ^ EDGE_CROSS))
+    nearer = moved(nearer, lambda lat, lon: (lat ^ 1, lon ^ EDGE_CROSS))
     return nearer + farther
 
 
@@ -207,21 +215,46 @@
         return (lax.all_gather(packed, "lon", axis=0),), False
     pieces = [packed]
     for apart in range(2, peers, 2):
-        pieces.append(swapped(packed, "lon", apart))
+        pieces.append(moved(packed, lambda lat, lon: (lat, lon ^ apart ^ CHIP_CROSS)))
     same = jnp.stack(pieces)
-    return (same, swapped(same, "lon", 1)), True
-
-
-def scattered(total):
-    peers = lax.axis_size("lat")
+    return (same, moved(same, lambda lat, lon: (lat, lon ^ 1))), True
+
+
+def sum_kernel(own_ref, *refs):
+    *piece_refs, state_hbm, flux_hbm, state_ref, flux_ref, sems = refs
+    value = own_ref[0]
+    for piece_ref in piece_refs:
+        value = value + piece_ref[0]
+    rows = state_ref.shape[0] * state_ref.shape[1]
+    state_ref[...] = value[:rows].reshape(state_ref.shape)
+    flux_ref[...] = value[rows:].reshape(flux_ref.shape)
+    copies = [pltpu.make_async_copy(state_ref, state_hbm, sems.at[0]), pltpu.make_async_copy(flux_ref, flux_hbm, sems.at[1])]
+    for copy in copies:
+        copy.start()
+    for copy in copies:
+        copy.wait()
+
+
+def scattered(total, levels):
+    peers, _, columns = total.shape
+    shapes = ((2, levels, 1, columns), (2, 1, columns))
     if peers > DIRECT:
-        return lax.psum_scatter(total, "lat", scatter_dimension=1, tiled=True)
+        value = lax.psum_scatter(total, "lat", scatter_dimension=0, tiled=True)[0]
+        return value[:16].reshape(shapes[0]), value[16:].reshape(shapes[1])
     me = lax.axis_index("lat")
-    kept = lax.dynamic_slice_in_dim(total, me, 1, 1)
+    pieces = [lax.dynamic_slice_in_dim(total, me, 1, 0)]
     for apart in range(1, peers):
-        piece = lax.dynamic_slice_in_dim(total, me ^ apart, 1, 1)
-        kept = kept + swapped(piece, "lat", apart)
-    return kept
+        piece = lax.dynamic_slice_in_dim(total, me ^ apart, 1, 0)
+        pieces.append(moved(piece, lambda lat, lon: (lat ^ apart, lon)))
+    return pl.pallas_call(
+        sum_kernel,
+        out_shape=[jax.ShapeDtypeStruct(shape, jnp.float32) for shape in shapes],
+        in_specs=[pl.BlockSpec(memory_space=pltpu.VMEM)] * peers,
+        out_specs=[pl.BlockSpec(memory_space=pltpu.HBM)] * 2,
+        scratch_shapes=[pltpu.VMEM(shape, jnp.float32) for shape in shapes] + [pltpu.SemaphoreType.DMA((2,))],
+        compiler_params=pltpu.CompilerParams(vmem_limit_bytes=GRANT),
+        name="total",
+    )(*pieces)
 
 
 def shards(forcing, zonal, meridional, mixing, panel):
@@ -230,10 +263,8 @@
     packed = jnp.concatenate([main, along_lat(nearer, farther)], 0)
     band, exchanged = gathered(packed)
     vectors, adjoint = band_vectors(band, rows, cols, lax.axis_size("lon"), exchanged)
-    total = jnp.einsum("rc,cam->ram", vectors, panel, preferred_element_type=jnp.float32)
-    summed = scattered(total)
-    state_grad = summed[:16].reshape(2, levels, 1, summed.shape[2])
-    flux_grad = summed[16:]
+    total = jnp.einsum("rc,cam->arm", vectors, panel, preferred_element_type=jnp.float32)
+    state_grad, flux_grad = scattered(total, levels)
     return (adjoint.reshape(2, levels, rows, cols), state_grad, flux_grad)
 
 

time: 32.3 us -> 28.7 us (0.89)
  starting transfers between devices: 15.8 us -> 13 us
  local copies, waits for them, and re-layouts: 2.01 us -> 0.84 us
  Pallas kernels: 2.9 us -> 3.53 us
    ppermute x9, starting transfers between devices: 15.8 us -> 13 us  [moved(): return lax.ppermute(value, ('lat', 'lon'), pairs)]
    slice x2 -> x0, local copies, waits for them, and re-layouts: 1.16 us -> none  [the longest x1 0.6 us: shards(): state_grad = summed[:16].reshape(2, levels, 1, summed.shape[2])]
    pallas_call x0 -> x1, Pallas kernels: none -> 0.63 us  [scattered(): pl.pallas_call(sum_kernel, out_shape=[jax.ShapeDtypeStruct(shape, jnp.flo...]
  transfers between devices with their start and end apart: 9 -> 9, of which waited for: 6 -> 5; matrix products, arithmetic and copies ran while one was open for 3% -> 3% of each run, Pallas kernels for 0% -> 0%
where the time goes in v3:
time: 28.7 us; the launch traced here: 28.5 us
  starting transfers between devices  13 us (45%)
  waiting for transfers between devices  10.2 us (36%)
  Pallas kernels  3.53 us (12%)
  local copies, waits for them, and re-layouts  0.84 us (3%)
  between operations  0.69 us (2%)
    ppermute x9, starting transfers between devices, moved(): return lax.ppermute(value, ('lat', 'lon'), pairs)  13 us
    ppermute x9, waiting for transfers between devices, moved(): return lax.ppermute(value, ('lat', 'lon'), pairs)  10.2 us
    pallas_call x1, Pallas kernels, packed_fields(): pl.pallas_call(functools.partial(pack_kernel, rows, cols), out_shape=(jax...  2.17 us
    unnamed x3, local copies, waits for them, and re-layouts  0.74 us
    pallas_call x1, Pallas kernels, band_vectors(): pl.pallas_call(functools.partial(band_kernel, rows, cols, blocks, exchang...  0.72 us
    pallas_call x1, Pallas kernels, scattered(): pl.pallas_call(sum_kernel, out_shape=[jax.ShapeDtypeStruct(shape, jnp.flo...  0.63 us
  transfers between devices with their start and end apart: 9, of which 5 were waited for; matrix products, arithmetic and copies ran while one was open for 3% of the time, Pallas kernels for 0%

profile of v3, /device:TPU:0, one launch (start us, length us, event | category | flops | bytes accessed | tf_op | source)
XLA Modules:
  0.0 28.5 jit_solution(17037593291937830679)
XLA Ops:
  0.6 0.0 copy-start
  0.6 2.2 %pack.1 = (f32[56,128]{1,0:T(8,128)S(1)}, f32[16,128]{1,0:T(8,128)S(1)}, f32[16,128]{1,0:T(8,128)S(1)}) custom-call(f32[2,2,8,8,16]{4,3,2,1,0:T(8,128)} %bitcast.20, f32[8,8,16]{2,1,0:T(8,128)} %bitcast.24, f32[8,8,16]{2,1,0:T(8,128)} %bitcast.25, f32[7,8,16]{2,1,0:T(8,128)} %bitcast.26), custom_call_target="tpu_custom_call" | custom-call | tf_op jit(solution)/shard_map/pack/pallas_call | solution.py:83
  2.8 2.5 %collective-permute-start = (f32[16,128]{1,0:T(8,128)S(1)}, f32[16,128]{1,0:T(8,128)S(1)}, u32[]{:S(2)}, u32[]{:S(2)}) collective-permute-start(f32[16,128]{1,0:T(8,128)S(1)} %get-tuple-element.11), channel_id=1, source_target_pairs={{0,9},{1,8},{2,11},{3,10},{4,13},{5,12},{6,15},{7,14},{8,1},{9,0},... | collective-permute-start | bytes 24584 | tf_op jit(solution)/shard_map/ppermute | solution.py:203
  5.3 1.8 %collective-permute-start.1 = (f32[16,128]{1,0:T(8,128)S(1)}, f32[16,128]{1,0:T(8,128)S(1)}, u32[]{:S(2)}, u32[]{:S(2)}) collective-permute-start(f32[16,128]{1,0:T(8,128)S(1)} %get-tuple-element.12), channel_id=1, source_target_pairs={{0,25},{1,24},{2,27},{3,26},{4,29},{5,28},{6,31},{7,30},{8,17},{9,... | collective-permute-start | bytes 24584 | tf_op jit(solution)/shard_map/ppermute | solution.py:203
  7.1 0.0 collective-permute-done
  7.1 2.2 %collective-permute-done.1 = f32[16,128]{1,0:T(8,128)S(1)} collective-permute-done((f32[16,128]{1,0:T(8,128)S(1)}, f32[16,128]{1,0:T(8,128)S(1)}, u32[]{:S(2)}, u32[]{:S(2)}) %collective-permute-start.1) | collective-permute-done | bytes 8224 | tf_op jit(solution)/shard_map/ppermute | solution.py:203
  9.3 1.9 %collective-permute-start.2 = (f32[72,128]{1,0:T(8,128)S(1)}, f32[72,128]{1,0:T(8,128)S(1)}, u32[]{:S(2)}, u32[]{:S(2)}) collective-permute-start(f32[72,128]{1,0:T(8,128)S(1)} %get-tuple-element.28), channel_id=1, source_target_pairs={{0,3},{1,2},{2,1},{3,0},{4,7},{5,6},{6,5},{7,4},{8,11},{9,10},{10,... | collective-permute-start | bytes 110600 | tf_op jit(solution)/shard_map/ppermute | solution.py:203
  11.2 2.0 %collective-permute-start.3 = (f32[72,128]{1,0:T(8,128)S(1)}, f32[72,128]{1,0:T(8,128)S(1)}, u32[]{:S(2)}, u32[]{:S(2)}) collective-permute-start(f32[72,128]{1,0:T(8,128)S(1)} %get-tuple-element.28), channel_id=1, source_target_pairs={{0,5},{1,4},{2,7},{3,6},{4,1},{5,0},{6,3},{7,2},{8,13},{9,12},{10,... | collective-permute-start | bytes 110600 | tf_op jit(solution)/shard_map/ppermute | solution.py:203
  13.2 0.5 %collective-permute-start.4 = (f32[72,128]{1,0:T(8,128)S(1)}, f32[72,128]{1,0:T(8,128)S(1)}, u32[]{:S(2)}, u32[]{:S(2)}) collective-permute-start(f32[72,128]{1,0:T(8,128)S(1)} %get-tuple-element.28), channel_id=1, source_target_pairs={{0,7},{1,6},{2,5},{3,4},{4,3},{5,2},{6,1},{7,0},{8,15},{9,14},{10,... | collective-permute-start | bytes 110600 | tf_op jit(solution)/shard_map/ppermute | solution.py:203
  13.7 0.0 collective-permute-done.2
  13.7 2.8 %collective-permute-done.3 = f32[72,128]{1,0:T(8,128)S(1)} collective-permute-done((f32[72,128]{1,0:T(8,128)S(1)}, f32[72,128]{1,0:T(8,128)S(1)}, u32[]{:S(2)}, u32[]{:S(2)}) %collective-permute-start.3) | collective-permute-done | bytes 36896 | tf_op jit(solution)/shard_map/ppermute | solution.py:203
  16.5 1.9 %collective-permute-done.4 = f32[72,128]{1,0:T(8,128)S(1)} collective-permute-done((f32[72,128]{1,0:T(8,128)S(1)}, f32[72,128]{1,0:T(8,128)S(1)}, u32[]{:S(2)}, u32[]{:S(2)}) %collective-permute-start.4) | collective-permute-done | bytes 36896 | tf_op jit(solution)/shard_map/ppermute | solution.py:203
  18.4 0.7 %collective-permute-start.5 = (f32[4,72,128]{2,1,0:T(8,128)S(1)}, f32[4,72,128]{2,1,0:T(8,128)S(1)}, u32[]{:S(2)}, u32[]{:S(2)}) collective-permute-start(f32[4,72,128]{2,1,0:T(8,128)S(1)} %pad_maximum_fusion.refs_0_), channel_id=1, source_target_pairs={{0,1},{1,0},{2,3},{3,2},{4,5},{5,4},{6,7},{7,6},{8,9},{9,8},{10,11... | collective-permute-start | bytes 442376 | tf_op jit(solution)/shard_map/ppermute | solution.py:203
  19.2 1.0 %collective-permute-done.5.refs_1_ = f32[4,72,128]{2,1,0:T(8,128)S(1)} collective-permute-done((f32[4,72,128]{2,1,0:T(8,128)S(1)}, f32[4,72,128]{2,1,0:T(8,128)S(1)}, u32[]{:S(2)}, u32[]{:S(2)}) %collective-permute-start.5) | collective-permute-done | bytes 147488 | tf_op jit(solution)/shard_map/ppermute | solution.py:203
  20.2 0.7 %band.1 = (bf16[18,1024]{1,0:T(8,128)(2,1)S(1)}, f32[16,128]{1,0:T(8,128)S(1)}) custom-call(f32[4,72,128]{2,1,0:T(8,128)S(1)} %pad_maximum_fusion.refs_0_, f32[4,72,128]{2,1,0:T(8,128)S(1)} %collective-permute-done.5.refs_1_), custom_call_target="tpu_custom_call" | custom-call | tf_op jit(solution)/shard_map/band/pallas_call | solution.py:185
  20.9 0.0 copy-done
  20.9 0.3 fusion
  21.2 0.6 %collective-permute-start.6 = (f32[1,18,128]{2,1,0:T(8,128)S(1)}, f32[1,18,128]{2,1,0:T(8,128)S(1)}, u32[]{:S(2)}, u32[]{:S(2)}) collective-permute-start(f32[1,18,128]{2,1,0:T(8,128)S(1)} %get-tuple-element.25), channel_id=1, source_target_pairs={{0,8},{1,9},{2,10},{3,11},{4,12},{5,13},{6,14},{7,15},{8,0},{9,1},... | collective-permute-start | bytes 27656 | tf_op jit(solution)/shard_map/ppermute | solution.py:203
  21.8 1.5 %collective-permute-start.7 = (f32[1,18,128]{2,1,0:T(8,128)S(1)}, f32[1,18,128]{2,1,0:T(8,128)S(1)}, u32[]{:S(2)}, u32[]{:S(2)}) collective-permute-start(f32[1,18,128]{2,1,0:T(8,128)S(1)} %get-tuple-element.24), channel_id=1, source_target_pairs={{0,16},{1,17},{2,18},{3,19},{4,20},{5,21},{6,22},{7,23},{8,24},{9,... | collective-permute-start | bytes 27656 | tf_op jit(solution)/shard_map/ppermute | solution.py:203
  23.3 1.4 %collective-permute-start.8 = (f32[1,18,128]{2,1,0:T(8,128)S(1)}, f32[1,18,128]{2,1,0:T(8,128)S(1)}, u32[]{:S(2)}, u32[]{:S(2)}) collective-permute-start(f32[1,18,128]{2,1,0:T(8,128)S(1)} %get-tuple-element.23), channel_id=1, source_target_pairs={{0,24},{1,25},{2,26},{3,27},{4,28},{5,29},{6,30},{7,31},{8,16},{9,... | collective-permute-start | bytes 27656 | tf_op jit(solution)/shard_map/ppermute | solution.py:203
  24.7 0.1 reshape.13
  24.9 0.7 %copy.11 = f32[2,8,16,8]{2,3,1,0:T(8,128)} copy(f32[2,8,16,8]{3,2,1,0:T(8,128)S(1)} %reshape.13) | data formatting | bytes 16384
  25.6 0.0 collective-permute-done.6.refs_0_
  25.6 0.0 collective-permute-done.7.refs_1_
  25.6 2.3 %collective-permute-done.8.refs_2_ = f32[1,18,128]{2,1,0:T(8,128)S(1)} collective-permute-done((f32[1,18,128]{2,1,0:T(8,128)S(1)}, f32[1,18,128]{2,1,0:T(8,128)S(1)}, u32[]{:S(2)}, u32[]{:S(2)}) %collective-permute-start.8) | collective-permute-done | bytes 9248 | tf_op jit(solution)/shard_map/ppermute | solution.py:203
  27.9 0.6 %total.1 = (f32[2,8,1,128]{3,2,1,0:T(1,128)}, f32[2,1,128]{2,1,0:T(1,128)}) custom-call(f32[1,18,128]{2,1,0:T(8,128)S(1)} %get-tuple-element.26.own_ref, f32[1,18,128]{2,1,0:T(8,128)S(1)} %collective-permute-done.6.refs_0_, f32[1,18,128]{2,1,0:T(8,128)S(1)} %collective-permute-done.7.refs_1_, f32[1,18,128]{2,1,0:T(8,128)S(1)} %collective-permute-done.8.refs_2_), custom_call_target="tpu_custom_call" | custom-call | tf_op jit(solution)/shard_map/total/pallas_call | solution.py:249
  (4 shorter events, 0.0 us)
Async XLA Ops:
  0.6 20.3 %copy-start = (bf16[1024,4,128]{2,1,0:T(4,128)(2,1)S(1)}, bf16[1024,4,128]{2,1,0:T(4,128)(2,1)}, u32[]{:S(2)}) copy-start(bf16[1024,4,128]{2,1,0:T(4,128)(2,1)} %param.9) | copy-start | bytes 3145732
  2.8 4.2 %collective-permute-start = (f32[16,128]{1,0:T(8,128)S(1)}, f32[16,128]{1,0:T(8,128)S(1)}, u32[]{:S(2)}, u32[]{:S(2)}) collective-permute-start(f32[16,128]{1,0:T(8,128)S(1)} %get-tuple-element.11), channel_id=1, source_target_pairs={{0,9},{1,8},{2,11},{3,10},{4,13},{5,12},{6,15},{7,14},{8,1},{9,0},... | collective-permute-start | bytes 24584 | tf_op jit(solution)/shard_map/ppermute | solution.py:203
  5.3 4.0 %collective-permute-start.1 = (f32[16,128]{1,0:T(8,128)S(1)}, f32[16,128]{1,0:T(8,128)S(1)}, u32[]{:S(2)}, u32[]{:S(2)}) collective-permute-start(f32[16,128]{1,0:T(8,128)S(1)} %get-tuple-element.12), channel_id=1, source_target_pairs={{0,25},{1,24},{2,27},{3,26},{4,29},{5,28},{6,31},{7,30},{8,17},{9,... | collective-permute-start | bytes 24584 | tf_op jit(solution)/shard_map/ppermute | solution.py:203
  9.3 4.5 %collective-permute-start.2 = (f32[72,128]{1,0:T(8,128)S(1)}, f32[72,128]{1,0:T(8,128)S(1)}, u32[]{:S(2)}, u32[]{:S(2)}) collective-permute-start(f32[72,128]{1,0:T(8,128)S(1)} %get-tuple-element.28), channel_id=1, source_target_pairs={{0,3},{1,2},{2,1},{3,0},{4,7},{5,6},{6,5},{7,4},{8,11},{9,10},{10,... | collective-permute-start | bytes 110600 | tf_op jit(solution)/shard_map/ppermute | solution.py:203
  11.2 5.3 %collective-permute-start.3 = (f32[72,128]{1,0:T(8,128)S(1)}, f32[72,128]{1,0:T(8,128)S(1)}, u32[]{:S(2)}, u32[]{:S(2)}) collective-permute-start(f32[72,128]{1,0:T(8,128)S(1)} %get-tuple-element.28), channel_id=1, source_target_pairs={{0,5},{1,4},{2,7},{3,6},{4,1},{5,0},{6,3},{7,2},{8,13},{9,12},{10,... | collective-permute-start | bytes 110600 | tf_op jit(solution)/shard_map/ppermute | solution.py:203
  13.2 5.2 %collective-permute-start.4 = (f32[72,128]{1,0:T(8,128)S(1)}, f32[72,128]{1,0:T(8,128)S(1)}, u32[]{:S(2)}, u32[]{:S(2)}) collective-permute-start(f32[72,128]{1,0:T(8,128)S(1)} %get-tuple-element.28), channel_id=1, source_target_pairs={{0,7},{1,6},{2,5},{3,4},{4,3},{5,2},{6,1},{7,0},{8,15},{9,14},{10,... | collective-permute-start | bytes 110600 | tf_op jit(solution)/shard_map/ppermute | solution.py:203
  18.4 1.7 %collective-permute-start.5 = (f32[4,72,128]{2,1,0:T(8,128)S(1)}, f32[4,72,128]{2,1,0:T(8,128)S(1)}, u32[]{:S(2)}, u32[]{:S(2)}) collective-permute-start(f32[4,72,128]{2,1,0:T(8,128)S(1)} %pad_maximum_fusion.refs_0_), channel_id=1, source_target_pairs={{0,1},{1,0},{2,3},{3,2},{4,5},{5,4},{6,7},{7,6},{8,9},{9,8},{10,11... | collective-permute-start | bytes 442376 | tf_op jit(solution)/shard_map/ppermute | solution.py:203
  21.2 4.4 %collective-permute-start.6 = (f32[1,18,128]{2,1,0:T(8,128)S(1)}, f32[1,18,128]{2,1,0:T(8,128)S(1)}, u32[]{:S(2)}, u32[]{:S(2)}) collective-permute-start(f32[1,18,128]{2,1,0:T(8,128)S(1)} %get-tuple-element.25), channel_id=1, source_target_pairs={{0,8},{1,9},{2,10},{3,11},{4,12},{5,13},{6,14},{7,15},{8,0},{9,1},... | collective-permute-start | bytes 27656 | tf_op jit(solution)/shard_map/ppermute | solution.py:203
  21.8 3.8 %collective-permute-start.7 = (f32[1,18,128]{2,1,0:T(8,128)S(1)}, f32[1,18,128]{2,1,0:T(8,128)S(1)}, u32[]{:S(2)}, u32[]{:S(2)}) collective-permute-start(f32[1,18,128]{2,1,0:T(8,128)S(1)} %get-tuple-element.24), channel_id=1, source_target_pairs={{0,16},{1,17},{2,18},{3,19},{4,20},{5,21},{6,22},{7,23},{8,24},{9,... | collective-permute-start | bytes 27656 | tf_op jit(solution)/shard_map/ppermute | solution.py:203
  23.3 4.6 %collective-permute-start.8 = (f32[1,18,128]{2,1,0:T(8,128)S(1)}, f32[1,18,128]{2,1,0:T(8,128)S(1)}, u32[]{:S(2)}, u32[]{:S(2)}) collective-permute-start(f32[1,18,128]{2,1,0:T(8,128)S(1)} %get-tuple-element.23), channel_id=1, source_target_pairs={{0,24},{1,25},{2,26},{3,27},{4,28},{5,29},{6,30},{7,31},{8,16},{9,... | collective-permute-start | bytes 27656 | tf_op jit(solution)/shard_map/ppermute | solution.py:203

commit v4 on v3

--- a/solution.py
+++ b/solution.py
@@ -3,6 +3,7 @@
 import jax.numpy as jnp
 from jax import lax
 from jax.experimental import pallas as pl
+from jax.experimental.layout import Layout, with_layout_constraint
 from jax.experimental.pallas import tpu as pltpu
 from jax.sharding import PartitionSpec as P
 
@@ -11,6 +12,7 @@
 GRANT = 4 << 20
 EDGE_CROSS = 1
 CHIP_CROSS = 1
+EARLY = (4,)
 
 
 def roll(value, shift, axis=-1):
@@ -209,13 +211,20 @@
     return nearer + farther
 
 
-def gathered(packed):
+def gathered(main, halo):
     peers = lax.axis_size("lon")
+    packed = jnp.concatenate([main, halo], 0)
     if peers > 2 * DIRECT:
         return (lax.all_gather(packed, "lon", axis=0),), False
     pieces = [packed]
     for apart in range(2, peers, 2):
-        pieces.append(moved(packed, lambda lat, lon: (lat, lon ^ apart ^ CHIP_CROSS)))
+        target = lambda lat, lon: (lat, lon ^ apart ^ CHIP_CROSS)
+        if apart in EARLY:
+            ahead = moved(main, target)
+            behind = moved(halo, target)
+            pieces.append(jnp.concatenate([ahead, behind], 0))
+        else:
+            pieces.append(moved(packed, target))
     same = jnp.stack(pieces)
     return (same, moved(same, lambda lat, lon: (lat, lon ^ 1))), True
 
@@ -235,17 +244,23 @@
         copy.wait()
 
 
-def scattered(total, levels):
-    peers, _, columns = total.shape
+def product(vectors, panel):
+    return jnp.einsum("rc,cam->arm", vectors, panel, preferred_element_type=jnp.float32)
+
+
+def scattered(vectors, panel, opposite, levels):
+    peers, columns = panel.shape[1:]
     shapes = ((2, levels, 1, columns), (2, 1, columns))
-    if peers > DIRECT:
-        value = lax.psum_scatter(total, "lat", scatter_dimension=0, tiled=True)[0]
+    if opposite is None:
+        value = lax.psum_scatter(product(vectors, panel), "lat", scatter_dimension=0, tiled=True)[0]
         return value[:16].reshape(shapes[0]), value[16:].reshape(shapes[1])
     me = lax.axis_index("lat")
-    pieces = [lax.dynamic_slice_in_dim(total, me, 1, 0)]
+    total = product(vectors, opposite)
+    own = product(vectors, panel)
+    pieces = [lax.dynamic_slice_in_dim(own, me, 1, 0)]
     for apart in range(1, peers):
         piece = lax.dynamic_slice_in_dim(total, me ^ apart, 1, 0)
-        pieces.append(moved(piece, lambda lat, lon: (lat ^ apart, lon)))
+        pieces.append(moved(piece, lambda lat, lon: (lat ^ apart, lon ^ 1)))
     return pl.pallas_call(
         sum_kernel,
         out_shape=[jax.ShapeDtypeStruct(shape, jnp.float32) for shape in shapes],
@@ -260,12 +275,15 @@
 def shards(forcing, zonal, meridional, mixing, panel):
     levels, rows, cols = zonal.shape
     main, nearer, farther = packed_fields(forcing, zonal, meridional, mixing)
-    packed = jnp.concatenate([main, along_lat(nearer, farther)], 0)
-    band, exchanged = gathered(packed)
+    opposite = None
+    if panel.shape[1] <= DIRECT:
+        opposite = moved(with_layout_constraint(panel, Layout((0, 1, 2))), lambda lat, lon: (lat, lon ^ 1))
+        opposite = with_layout_constraint(opposite, Layout((0, 1, 2)))
+    band, exchanged = gathered(main, along_lat(nearer, farther))
     vectors, adjoint = band_vectors(band, rows, cols, lax.axis_size("lon"), exchanged)
-    total = jnp.einsum("rc,cam->arm", vectors, panel, preferred_element_type=jnp.float32)
-    state_grad, flux_grad = scattered(total, levels)
-    return (adjoint.reshape(2, levels, rows, cols), state_grad, flux_grad)
+    state_grad, flux_grad = scattered(vectors, panel, opposite, levels)
+    adjoint_state = adjoint.reshape(2, levels, rows, cols)
+    return (adjoint_state, state_grad, flux_grad)
 
 
 def solution(mesh):

time: 28.7 us -> 28.4 us (0.990)
  waiting for transfers between devices: 10.2 us -> 8.65 us
  starting transfers between devices: 13 us -> 14.1 us
    ppermute x9 -> x11, waiting for transfers between devices: 10.2 us -> 8.65 us  [moved(): return lax.ppermute(value, ('lat', 'lon'), pairs)]
    ppermute x9 -> x11, starting transfers between devices: 13 us -> 14.1 us  [moved(): return lax.ppermute(value, ('lat', 'lon'), pairs)]
  transfers between devices with their start and end apart: 9 -> 11, of which waited for: 5 -> 8; matrix products, arithmetic and copies ran while one was open for 3% -> 4% of each run, Pallas kernels for 0% -> 10%
where the time goes in v4:
time: 28.4 us; the launch traced here: 28.3 us
  starting transfers between devices  14.1 us (50%)
  waiting for transfers between devices  8.65 us (30%)
  Pallas kernels  3.44 us (12%)
  local copies, waits for them, and re-layouts  0.84 us (3%)
  between operations  0.7 us (2%)
  matrix products  0.51 us (2%)
    ppermute x11, starting transfers between devices, moved(): return lax.ppermute(value, ('lat', 'lon'), pairs)  14.1 us
    ppermute x11, waiting for transfers between devices, moved(): return lax.ppermute(value, ('lat', 'lon'), pairs)  8.65 us
    pallas_call x1, Pallas kernels, packed_fields(): pl.pallas_call(functools.partial(pack_kernel, rows, cols), out_shape=(jax...  2.09 us
    unnamed x3, local copies, waits for them, and re-layouts  0.73 us
    pallas_call x1, Pallas kernels, band_vectors(): pl.pallas_call(functools.partial(band_kernel, rows, cols, blocks, exchang...  0.72 us
    pallas_call x1, Pallas kernels, scattered(): pl.pallas_call(sum_kernel, out_shape=[jax.ShapeDtypeStruct(shape, jnp.flo...  0.63 us
  transfers between devices with their start and end apart: 11, of which 8 were waited for; matrix products, arithmetic and copies ran while one was open for 4% of the time, Pallas kernels for 10%

profile of v4, /device:TPU:0, one launch (start us, length us, event | category | flops | bytes accessed | tf_op | source)
XLA Modules:
  0.0 28.3 jit_solution(2229847455061802772)
XLA Ops:
  0.6 0.0 copy-start
  0.6 0.6 %collective-permute-start.7 = (bf16[1024,4,128]{2,1,0:T(4,128)(2,1)}, bf16[1024,4,128]{2,1,0:T(4,128)(2,1)S(1)}, u32[]{:S(2)}, u32[]{:S(2)}) collective-permute-start(bf16[1024,4,128]{2,1,0:T(4,128)(2,1)} %param.9), channel_id=1, source_target_pairs={{0,1},{1,0},{2,3},{3,2},{4,5},{5,4},{6,7},{7,6},{8,9},{9,8},{10,11... | collective-permute-start | bytes 3145736 | tf_op jit(solution)/shard_map/ppermute | solution.py:205
  1.2 2.1 %pack.1 = (f32[56,128]{1,0:T(8,128)S(1)}, f32[16,128]{1,0:T(8,128)S(1)}, f32[16,128]{1,0:T(8,128)S(1)}) custom-call(f32[2,2,8,8,16]{4,3,2,1,0:T(8,128)} %bitcast.23, f32[8,8,16]{2,1,0:T(8,128)} %bitcast.26, f32[8,8,16]{2,1,0:T(8,128)} %bitcast.27, f32[7,8,16]{2,1,0:T(8,128)} %bitcast.28), custom_call_target="tpu_custom_call" | custom-call | tf_op jit(solution)/shard_map/pack/pallas_call | solution.py:85
  3.3 2.7 %collective-permute-start = (f32[16,128]{1,0:T(8,128)S(1)}, f32[16,128]{1,0:T(8,128)S(1)}, u32[]{:S(2)}, u32[]{:S(2)}) collective-permute-start(f32[16,128]{1,0:T(8,128)S(1)} %get-tuple-element.11), channel_id=1, source_target_pairs={{0,9},{1,8},{2,11},{3,10},{4,13},{5,12},{6,15},{7,14},{8,1},{9,0},... | collective-permute-start | bytes 24584 | tf_op jit(solution)/shard_map/ppermute | solution.py:205
  5.9 1.2 %collective-permute-start.1 = (f32[16,128]{1,0:T(8,128)S(1)}, f32[16,128]{1,0:T(8,128)S(1)}, u32[]{:S(2)}, u32[]{:S(2)}) collective-permute-start(f32[16,128]{1,0:T(8,128)S(1)} %get-tuple-element.12), channel_id=1, source_target_pairs={{0,25},{1,24},{2,27},{3,26},{4,29},{5,28},{6,31},{7,30},{8,17},{9,... | collective-permute-start | bytes 24584 | tf_op jit(solution)/shard_map/ppermute | solution.py:205
  7.1 2.6 %collective-permute-start.3 = (f32[56,128]{1,0:T(8,128)S(1)}, f32[56,128]{1,0:T(8,128)S(1)}, u32[]{:S(2)}, u32[]{:S(2)}) collective-permute-start(f32[56,128]{1,0:T(8,128)S(1)} %get-tuple-element.10), channel_id=1, source_target_pairs={{0,5},{1,4},{2,7},{3,6},{4,1},{5,0},{6,3},{7,2},{8,13},{9,12},{10,... | collective-permute-start | bytes 86024 | tf_op jit(solution)/shard_map/ppermute | solution.py:205
  9.7 0.0 collective-permute-done
  9.8 0.2 collective-permute-done.1
  9.9 2.3 %collective-permute-start.4 = (f32[16,128]{1,0:T(8,128)S(1)}, f32[16,128]{1,0:T(8,128)S(1)}, u32[]{:S(2)}, u32[]{:S(2)}) collective-permute-start(f32[16,128]{1,0:T(8,128)S(1)} %add.15), channel_id=1, source_target_pairs={{0,5},{1,4},{2,7},{3,6},{4,1},{5,0},{6,3},{7,2},{8,13},{9,12},{10,... | collective-permute-start | bytes 24584 | tf_op jit(solution)/shard_map/ppermute | solution.py:205
  12.2 1.6 %collective-permute-start.2 = (f32[72,128]{1,0:T(8,128)S(1)}, f32[72,128]{1,0:T(8,128)S(1)}, u32[]{:S(2)}, u32[]{:S(2)}) collective-permute-start(f32[72,128]{1,0:T(8,128)S(1)} %get-tuple-element.27), channel_id=1, source_target_pairs={{0,3},{1,2},{2,1},{3,0},{4,7},{5,6},{6,5},{7,4},{8,11},{9,10},{10,... | collective-permute-start | bytes 110600 | tf_op jit(solution)/shard_map/ppermute | solution.py:205
  13.8 0.0 collective-permute-start.5
  13.8 0.1 collective-permute-done.4
  13.9 0.0 collective-permute-done.3
  13.9 1.7 %collective-permute-done.2 = f32[72,128]{1,0:T(8,128)S(1)} collective-permute-done((f32[72,128]{1,0:T(8,128)S(1)}, f32[72,128]{1,0:T(8,128)S(1)}, u32[]{:S(2)}, u32[]{:S(2)}) %collective-permute-start.2) | collective-permute-done | bytes 36896 | tf_op jit(solution)/shard_map/ppermute | solution.py:205
  15.6 3.5 %collective-permute-done.5 = f32[72,128]{1,0:T(8,128)S(1)} collective-permute-done((f32[72,128]{1,0:T(8,128)S(1)}, f32[72,128]{1,0:T(8,128)S(1)}, u32[]{:S(2)}, u32[]{:S(2)}) %collective-permute-start.5) | collective-permute-done | bytes 36896 | tf_op jit(solution)/shard_map/ppermute | solution.py:205
  19.1 0.2 collective-permute-start.6
  19.3 1.3 %collective-permute-done.6.refs_1_ = f32[4,72,128]{2,1,0:T(8,128)S(1)} collective-permute-done((f32[4,72,128]{2,1,0:T(8,128)S(1)}, f32[4,72,128]{2,1,0:T(8,128)S(1)}, u32[]{:S(2)}, u32[]{:S(2)}) %collective-permute-start.6) | collective-permute-done | bytes 147488 | tf_op jit(solution)/shard_map/ppermute | solution.py:205
  20.6 0.7 %band.1 = (bf16[18,1024]{1,0:T(8,128)(2,1)S(1)}, f32[16,128]{1,0:T(8,128)S(1)}) custom-call(f32[4,72,128]{2,1,0:T(8,128)S(1)} %pad_maximum_fusion.refs_0_, f32[4,72,128]{2,1,0:T(8,128)S(1)} %collective-permute-done.6.refs_1_), custom_call_target="tpu_custom_call" | custom-call | tf_op jit(solution)/shard_map/band/pallas_call | solution.py:187
  21.3 0.0 copy-done
  21.3 0.3 fusion.2
  21.5 0.0 collective-permute-done.7
  21.6 0.3 fusion
  21.8 1.3 %collective-permute-start.10 = (f32[1,18,128]{2,1,0:T(8,128)S(1)}, f32[1,18,128]{2,1,0:T(8,128)S(1)}, u32[]{:S(2)}, u32[]{:S(2)}) collective-permute-start(f32[1,18,128]{2,1,0:T(8,128)S(1)} %get-tuple-element.23), channel_id=1, source_target_pairs={{0,25},{1,24},{2,27},{3,26},{4,29},{5,28},{6,31},{7,30},{8,17},{9,... | collective-permute-start | bytes 27656 | tf_op jit(solution)/shard_map/ppermute | solution.py:205
  23.1 1.4 %collective-permute-start.8 = (f32[1,18,128]{2,1,0:T(8,128)S(1)}, f32[1,18,128]{2,1,0:T(8,128)S(1)}, u32[]{:S(2)}, u32[]{:S(2)}) collective-permute-start(f32[1,18,128]{2,1,0:T(8,128)S(1)} %get-tuple-element.25), channel_id=1, source_target_pairs={{0,9},{1,8},{2,11},{3,10},{4,13},{5,12},{6,15},{7,14},{8,1},{9,0},... | collective-permute-start | bytes 27656 | tf_op jit(solution)/shard_map/ppermute | solution.py:205
  24.5 0.3 %collective-permute-start.9 = (f32[1,18,128]{2,1,0:T(8,128)S(1)}, f32[1,18,128]{2,1,0:T(8,128)S(1)}, u32[]{:S(2)}, u32[]{:S(2)}) collective-permute-start(f32[1,18,128]{2,1,0:T(8,128)S(1)} %get-tuple-element.24), channel_id=1, source_target_pairs={{0,17},{1,16},{2,19},{3,18},{4,21},{5,20},{6,23},{7,22},{8,25},{9,... | collective-permute-start | bytes 27656 | tf_op jit(solution)/shard_map/ppermute | solution.py:205
  24.9 0.1 reshape.13
  25.0 0.7 %copy.13 = f32[2,8,16,8]{2,3,1,0:T(8,128)} copy(f32[2,8,16,8]{3,2,1,0:T(8,128)S(1)} %reshape.13) | data formatting | bytes 16384
  25.7 0.2 collective-permute-done.10.refs_2_
  25.9 0.3 %collective-permute-done.8.refs_0_ = f32[1,18,128]{2,1,0:T(8,128)S(1)} collective-permute-done((f32[1,18,128]{2,1,0:T(8,128)S(1)}, f32[1,18,128]{2,1,0:T(8,128)S(1)}, u32[]{:S(2)}, u32[]{:S(2)}) %collective-permute-start.8) | collective-permute-done | bytes 9248 | tf_op jit(solution)/shard_map/ppermute | solution.py:205
  26.3 1.4 %collective-permute-done.9.refs_1_ = f32[1,18,128]{2,1,0:T(8,128)S(1)} collective-permute-done((f32[1,18,128]{2,1,0:T(8,128)S(1)}, f32[1,18,128]{2,1,0:T(8,128)S(1)}, u32[]{:S(2)}, u32[]{:S(2)}) %collective-permute-start.9) | collective-permute-done | bytes 9248 | tf_op jit(solution)/shard_map/ppermute | solution.py:205
  27.6 0.6 %total.1 = (f32[2,8,1,128]{3,2,1,0:T(1,128)}, f32[2,1,128]{2,1,0:T(1,128)}) custom-call(f32[1,18,128]{2,1,0:T(8,128)S(1)} %dynamic-slice_bitcast_fusion.3.own_ref, f32[1,18,128]{2,1,0:T(8,128)S(1)} %collective-permute-done.8.refs_0_, f32[1,18,128]{2,1,0:T(8,128)S(1)} %collective-permute-done.9.refs_1_, f32[1,18,128]{2,1,0:T(8,128)S(1)} %collective-permute-done.10.refs_2_), custom_call_target="tpu_custom_call" | custom-call | tf_op jit(solution)/shard_map/total/pallas_call | solution.py:264
  (6 shorter events, 0.0 us)
Async XLA Ops:
  0.6 20.7 %copy-start = (bf16[1024,4,128]{2,1,0:T(4,128)(2,1)S(1)}, bf16[1024,4,128]{2,1,0:T(4,128)(2,1)}, u32[]{:S(2)}) copy-start(bf16[1024,4,128]{2,1,0:T(4,128)(2,1)} %param.9) | copy-start | bytes 3145732
  0.6 20.9 %collective-permute-start.7 = (bf16[1024,4,128]{2,1,0:T(4,128)(2,1)}, bf16[1024,4,128]{2,1,0:T(4,128)(2,1)S(1)}, u32[]{:S(2)}, u32[]{:S(2)}) collective-permute-start(bf16[1024,4,128]{2,1,0:T(4,128)(2,1)} %param.9), channel_id=1, source_target_pairs={{0,1},{1,0},{2,3},{3,2},{4,5},{5,4},{6,7},{7,6},{8,9},{9,8},{10,11... | collective-permute-start | bytes 3145736 | tf_op jit(solution)/shard_map/ppermute | solution.py:205
  3.3 6.5 %collective-permute-start = (f32[16,128]{1,0:T(8,128)S(1)}, f32[16,128]{1,0:T(8,128)S(1)}, u32[]{:S(2)}, u32[]{:S(2)}) collective-permute-start(f32[16,128]{1,0:T(8,128)S(1)} %get-tuple-element.11), channel_id=1, source_target_pairs={{0,9},{1,8},{2,11},{3,10},{4,13},{5,12},{6,15},{7,14},{8,1},{9,0},... | collective-permute-start | bytes 24584 | tf_op jit(solution)/shard_map/ppermute | solution.py:205
  5.9 4.0 %collective-permute-start.1 = (f32[16,128]{1,0:T(8,128)S(1)}, f32[16,128]{1,0:T(8,128)S(1)}, u32[]{:S(2)}, u32[]{:S(2)}) collective-permute-start(f32[16,128]{1,0:T(8,128)S(1)} %get-tuple-element.12), channel_id=1, source_target_pairs={{0,25},{1,24},{2,27},{3,26},{4,29},{5,28},{6,31},{7,30},{8,17},{9,... | collective-permute-start | bytes 24584 | tf_op jit(solution)/shard_map/ppermute | solution.py:205
  7.1 6.8 %collective-permute-start.3 = (f32[56,128]{1,0:T(8,128)S(1)}, f32[56,128]{1,0:T(8,128)S(1)}, u32[]{:S(2)}, u32[]{:S(2)}) collective-permute-start(f32[56,128]{1,0:T(8,128)S(1)} %get-tuple-element.10), channel_id=1, source_target_pairs={{0,5},{1,4},{2,7},{3,6},{4,1},{5,0},{6,3},{7,2},{8,13},{9,12},{10,... | collective-permute-start | bytes 86024 | tf_op jit(solution)/shard_map/ppermute | solution.py:205
  9.9 4.0 %collective-permute-start.4 = (f32[16,128]{1,0:T(8,128)S(1)}, f32[16,128]{1,0:T(8,128)S(1)}, u32[]{:S(2)}, u32[]{:S(2)}) collective-permute-start(f32[16,128]{1,0:T(8,128)S(1)} %add.15), channel_id=1, source_target_pairs={{0,5},{1,4},{2,7},{3,6},{4,1},{5,0},{6,3},{7,2},{8,13},{9,12},{10,... | collective-permute-start | bytes 24584 | tf_op jit(solution)/shard_map/ppermute | solution.py:205
  12.2 3.4 %collective-permute-start.2 = (f32[72,128]{1,0:T(8,128)S(1)}, f32[72,128]{1,0:T(8,128)S(1)}, u32[]{:S(2)}, u32[]{:S(2)}) collective-permute-start(f32[72,128]{1,0:T(8,128)S(1)} %get-tuple-element.27), channel_id=1, source_target_pairs={{0,3},{1,2},{2,1},{3,0},{4,7},{5,6},{6,5},{7,4},{8,11},{9,10},{10,... | collective-permute-start | bytes 110600 | tf_op jit(solution)/shard_map/ppermute | solution.py:205
  13.8 5.3 %collective-permute-start.5 = (f32[72,128]{1,0:T(8,128)S(1)}, f32[72,128]{1,0:T(8,128)S(1)}, u32[]{:S(2)}, u32[]{:S(2)}) collective-permute-start(f32[72,128]{1,0:T(8,128)S(1)} %get-tuple-element.27), channel_id=1, source_target_pairs={{0,7},{1,6},{2,5},{3,4},{4,3},{5,2},{6,1},{7,0},{8,15},{9,14},{10,... | collective-permute-start | bytes 110600 | tf_op jit(solution)/shard_map/ppermute | solution.py:205
  19.1 1.4 %collective-permute-start.6 = (f32[4,72,128]{2,1,0:T(8,128)S(1)}, f32[4,72,128]{2,1,0:T(8,128)S(1)}, u32[]{:S(2)}, u32[]{:S(2)}) collective-permute-start(f32[4,72,128]{2,1,0:T(8,128)S(1)} %pad_maximum_fusion.refs_0_), channel_id=1, source_target_pairs={{0,1},{1,0},{2,3},{3,2},{4,5},{5,4},{6,7},{7,6},{8,9},{9,8},{10,11... | collective-permute-start | bytes 442376 | tf_op jit(solution)/shard_map/ppermute | solution.py:205
  21.8 4.1 %collective-permute-start.10 = (f32[1,18,128]{2,1,0:T(8,128)S(1)}, f32[1,18,128]{2,1,0:T(8,128)S(1)}, u32[]{:S(2)}, u32[]{:S(2)}) collective-permute-start(f32[1,18,128]{2,1,0:T(8,128)S(1)} %get-tuple-element.23), channel_id=1, source_target_pairs={{0,25},{1,24},{2,27},{3,26},{4,29},{5,28},{6,31},{7,30},{8,17},{9,... | collective-permute-start | bytes 27656 | tf_op jit(solution)/shard_map/ppermute | solution.py:205
  23.1 3.1 %collective-permute-start.8 = (f32[1,18,128]{2,1,0:T(8,128)S(1)}, f32[1,18,128]{2,1,0:T(8,128)S(1)}, u32[]{:S(2)}, u32[]{:S(2)}) collective-permute-start(f32[1,18,128]{2,1,0:T(8,128)S(1)} %get-tuple-element.25), channel_id=1, source_target_pairs={{0,9},{1,8},{2,11},{3,10},{4,13},{5,12},{6,15},{7,14},{8,1},{9,0},... | collective-permute-start | bytes 27656 | tf_op jit(solution)/shard_map/ppermute | solution.py:205
  24.5 3.1 %collective-permute-start.9 = (f32[1,18,128]{2,1,0:T(8,128)S(1)}, f32[1,18,128]{2,1,0:T(8,128)S(1)}, u32[]{:S(2)}, u32[]{:S(2)}) collective-permute-start(f32[1,18,128]{2,1,0:T(8,128)S(1)} %get-tuple-element.24), channel_id=1, source_target_pairs={{0,17},{1,16},{2,19},{3,18},{4,21},{5,20},{6,23},{7,22},{8,25},{9,... | collective-permute-start | bytes 27656 | tf_op jit(solution)/shard_map/ppermute | solution.py:205

commit v5 on v4

--- a/solution.py
+++ b/solution.py
@@ -22,6 +22,7 @@
 
 def pack_kernel(rows, cols, forcing_hbm, zonal_hbm, merid_hbm, mixing_hbm, main_ref, near_ref, far_ref,
                 forcing_ref, zonal_ref, merid_ref, mixing_ref, sems):
+    levels = zonal_hbm.shape[0] // cols
     copies = [
         pltpu.make_async_copy(source, target, sems.at[i])
         for i, (source, target) in enumerate(
@@ -30,46 +31,35 @@
     for copy in copies:
         copy.start()
     cells = rows * cols
-    two = 2 * cols
     lane = lax.broadcasted_iota(jnp.int32, (2, 8, cells), 2)
-    level = lax.broadcasted_iota(jnp.int32, (2, 8, cells), 1)
-    half = lax.broadcasted_iota(jnp.int32, (2, 8, cells), 0)
-    group = lane // cols
-    plane = half * 8 + level
-
-    def flat(planes):
-        value = planes.reshape(16 * cols, rows).T.reshape(2, 8, cells)
-        for step in (1, 2, 4):
-            upper = roll(roll(value, -step, 1), step * cols)
-            lower = roll(roll(value, step, 1), -step * cols)
-            here, there = (plane // step) % 2, (group // step) % 2
-            value = jnp.where(here == there, value, jnp.where(here == 0, upper, lower))
-        crossed = jnp.concatenate([value[1:], value[:1]], 0)
-        crossed = roll(crossed, 8 * cols)
-        return jnp.where(half == group // 8, value, crossed)
+    row = lane % rows
+
+    def flat(ref, start, count=levels):
+        pieces = [ref[pl.ds(start * cols + column, count, stride=cols), :] for column in range(cols)]
+        return jnp.concatenate(pieces, 1)
 
     copies[0].wait()
-    forced = flat(forcing_ref[1].reshape(16, cols, rows))
-    first = flat(forcing_ref[0].reshape(16, cols, rows))
+    first = jnp.stack([flat(forcing_ref, 0), flat(forcing_ref, levels)])
+    forced = jnp.stack([flat(forcing_ref, 2 * levels), flat(forcing_ref, 3 * levels)])
     copies[1].wait()
     copies[3].wait()
-    pair = flat(jnp.concatenate([zonal_ref[...], mixing_ref[...], jnp.zeros((1, cols, rows), jnp.float32)], 0))
+    mixing = jnp.concatenate([flat(mixing_ref, 0, levels - 1), jnp.zeros((1, cells), jnp.float32)], 0)
+    pair = jnp.stack([flat(zonal_ref, 0), mixing])
     copies[2].wait()
-    merid = merid_ref[...]
-    lone = flat(jnp.concatenate([merid, jnp.zeros_like(merid)], 0))
     place = lax.axis_index("lat")
     top = jnp.where(place == lax.axis_size("lat") - 1, 1, 0)
-    lone = jnp.where((group == rows - 1) & (top == 1), 0.0, lone)
+    merid = jnp.where((row[0] == rows - 1) & (top == 1), 0.0, flat(merid_ref, 0))
+    lone = jnp.stack([merid, jnp.zeros_like(merid)])
     main_ref[0:16] = forced.reshape(16, cells)
     main_ref[16:32] = first.reshape(16, cells)
     main_ref[32:48] = pair.reshape(16, cells)
-    main_ref[48:56] = lone[0]
+    main_ref[48:56] = merid
     upper = jnp.zeros((2, 8, cells), jnp.float32)
     lower = jnp.zeros((2, 8, cells), jnp.float32)
     for i, value in enumerate((forced, first, pair, lone)):
-        start = 2 * two * i
-        lower = jnp.where((lane >= start) & (lane < start + two), roll(value, start), lower)
-        upper = jnp.where((lane >= start + two) & (lane < start + 2 * two), roll(value, start + 2 * two), upper)
+        start = 4 * i
+        lower = jnp.where((row >= start) & (row < start + 2), roll(value, start), lower)
+        upper = jnp.where((row >= start + 2) & (row < start + 4), roll(value, start + 4 - rows), upper)
     even = place % 2 == 0
     near_ref[...] = jnp.where(even, upper, lower).reshape(16, cells)
     ended = (place == 0) | ((place == lax.axis_size("lat") - 1) & ~even)
@@ -79,15 +69,15 @@
 def packed_fields(forcing, zonal, meridional, mixing):
     _, rows, cols = zonal.shape
     cells = rows * cols
-    fields = (forcing, zonal, meridional, mixing)
-    values = [pltpu.with_memory_space_constraint(jnp.swapaxes(v, -1, -2), pltpu.HBM) for v in fields]
+    fields = [jnp.swapaxes(v, -1, -2).reshape(-1, rows) for v in (forcing, zonal, meridional, mixing)]
+    values = [pltpu.with_memory_space_constraint(v, pltpu.HBM) for v in fields]
     edge = jax.ShapeDtypeStruct((16, cells), jnp.float32)
     return pl.pallas_call(
         functools.partial(pack_kernel, rows, cols),
         out_shape=(jax.ShapeDtypeStruct((56, cells), jnp.float32), edge, edge),
         in_specs=[pl.BlockSpec(memory_space=pltpu.HBM)] * 4,
         out_specs=[pl.BlockSpec(memory_space=pltpu.VMEM)] * 3,
-        scratch_shapes=[pltpu.VMEM(v.shape, jnp.float32) for v in values] + [pltpu.SemaphoreType.DMA((4,))],
+        scratch_shapes=[pltpu.VMEM(v.shape, jnp.float32) for v in fields] + [pltpu.SemaphoreType.DMA((4,))],
         compiler_params=pltpu.CompilerParams(vmem_limit_bytes=GRANT),
         name="pack",
     )(*values)
@@ -97,7 +87,6 @@
     *band_refs, vec_ref, adjoint_ref, all_ref = refs
     me = lax.axis_index("lon")
     cells = rows * cols
-    two = 2 * cols
     mains, halos = [], []
     if exchanged:
         same, other = band_refs
@@ -118,28 +107,43 @@
     forced, first, zonal, merid, mixing = field(0, 2), field(16, 2), field(32, 1), field(48, 1), field(40, 1)
     halo = jnp.stack([block.reshape(2, 8, cells) for block in halos])
     lane = lax.broadcasted_iota(jnp.int32, (1, 1, 8, cells), 3)
-    column = lane % cols
-
-    def tile(main, source, place):
-        beyond = roll(source, two - place * 2 * two)
-        return jnp.where(lane < two, roll(main, two), jnp.where(lane < 3 * two, beyond, roll(main, 3 * two)))
+    row = lane % rows
+
+    def slots(main, source, place, base):
+        beyond = roll(source, base + 2 - 4 * place)
+        value = jnp.where(row < base + 6, beyond, roll(main, base + 6))
+        return jnp.where(row < base + 2, roll(main, base + 2 - rows), value)
+
+    def joined(main, source, place):
+        value = slots(main[:, :1], source[:, :1], place, 0)
+        return jnp.where(row < 8, value, slots(main[:, 1:], source[:, 1:], place, 8))
+
+    def doubled(main, source, place):
+        value = slots(main, source, place, 0)
+        return jnp.where(row < 8, value, roll(value, 8))
 
     def rotated(value, by):
         return jnp.concatenate([value[by:], value[:by]], 0)
 
     def east(value):
-        return jnp.where(column == cols - 1, roll(rotated(value, 1), cols - 1), roll(value, -1))
+        turned = roll(value, -rows)
+        return jnp.where(lane >= cells - rows, rotated(turned, 1), turned)
 
     def west(value):
-        return jnp.where(column == 0, roll(rotated(value, -1), 1 - cols), roll(value, 1))
+        turned = roll(value, rows)
+        return jnp.where(lane < rows, rotated(turned, -1), turned)
 
     def north(value, edge=None):
-        moved = roll(value, -cols)
-        return moved if edge is None else jnp.where(lane >= cells - cols, roll(edge, -3 * cols), moved)
+        turned = roll(value, -1)
+        return turned if edge is None else jnp.where(row == rows - 1, apart(edge, value, rows - 3, rows - 11), turned)
 
     def south(value, edge=None):
-        moved = roll(value, cols)
-        return moved if edge is None else jnp.where(lane < cols, roll(edge, -5 * cols), moved)
+        turned = roll(value, 1)
+        return turned if edge is None else jnp.where(row == 0, apart(edge, value, -5, -13), turned)
+
+    def apart(edge, value, one, another):
+        pieces = [roll(edge, shift) for shift in (one, another)[: value.shape[1]]]
+        return jnp.concatenate(pieces, 1)
 
     def diffuse(value, mix):
         flow = mix * (roll(value, -1, -2) - value)
@@ -157,11 +161,11 @@
         return (value * centre + east(value) * out_east - west(value) * in_west
                 + north(value, edge) * out_north - south(value, edge) * in_south)
 
-    forced_tile = tile(forced, halo, 0)
-    first_tile = tile(first, halo, 1)
-    zonal_tile = tile(zonal, halo[:, :1], 2)
-    mixing_tile = tile(mixing, halo[:, 1:], 2)
-    merid_tile = tile(merid, halo[:, :1], 3)
+    forced_tile = joined(forced, halo, 0)
+    first_tile = joined(first, halo, 1)
+    zonal_tile = doubled(zonal, halo[:, :1], 2)
+    mixing_tile = doubled(mixing, halo[:, 1:], 2)
+    merid_tile = doubled(merid, halo[:, :1], 3)
     main_factor = factors(zonal, merid, merid_tile)
     tile_factor = factors(zonal_tile, merid_tile)
     started = diffuse(forced, mixing)
@@ -171,15 +175,20 @@
     mixed = diffuse(middle, mixing)
     mixed_tile = diffuse(middle_tile, mixing_tile)
     adjoint = advect(mixed, main_factor, mixed_tile)
-    surface = forced + middle
+    surface = forced[:, :, :1] + middle[:, :, :1]
+    for block in range(blocks):
+        all_ref[block] = adjoint[block].reshape(16, cells)
+    adjoint_ref[...] = all_ref[me]
+    source = lax.broadcasted_iota(jnp.int32, (cells, cells), 0)
+    target = lax.broadcasted_iota(jnp.int32, (cells, cells), 1)
+    order = jnp.where(source == (target % cols) * rows + target // cols, 1.0, 0.0).astype(jnp.bfloat16)
+    fluxes = [surface[block, species] for block in range(blocks) for species in range(2)]
+    stacked = jnp.concatenate([adjoint.reshape(16 * blocks, cells)] + fluxes, 0).astype(jnp.bfloat16)
+    ordered = jnp.dot(stacked, order, preferred_element_type=jnp.float32).astype(jnp.bfloat16)
     for block in range(blocks):
         span = slice(block * cells, (block + 1) * cells)
-        own = adjoint[block].reshape(16, cells)
-        all_ref[block] = own
-        vec_ref[:16, span] = own.astype(jnp.bfloat16)
-        pair = jnp.concatenate([surface[block, 0, :1], surface[block, 1, :1]], 0)
-        vec_ref[16:18, span] = pair.astype(jnp.bfloat16)
-    adjoint_ref[...] = all_ref[me]
+        vec_ref[:16, span] = ordered[16 * block : 16 * block + 16]
+        vec_ref[16:18, span] = ordered[16 * blocks + 2 * block : 16 * blocks + 2 * block + 2]
 
 
 def band_vectors(band, rows, cols, blocks, exchanged):
@@ -282,7 +291,7 @@
     band, exchanged = gathered(main, along_lat(nearer, farther))
     vectors, adjoint = band_vectors(band, rows, cols, lax.axis_size("lon"), exchanged)
     state_grad, flux_grad = scattered(vectors, panel, opposite, levels)
-    adjoint_state = adjoint.reshape(2, levels, rows, cols)
+    adjoint_state = jnp.swapaxes(adjoint.reshape(2, levels, cols, rows), 2, 3)
     return (adjoint_state, state_grad, flux_grad)
 
 

time: 28.4 us -> 26.6 us (0.937)
  waiting for transfers between devices: 8.65 us -> 6.88 us
  starting transfers between devices: 14.1 us -> 14.9 us
  Pallas kernels: 3.44 us -> 2.81 us
    ppermute x11, waiting for transfers between devices: 8.65 us -> 6.88 us  [moved(): return lax.ppermute(value, ('lat', 'lon'), pairs)]
    pallas_call x1, Pallas kernels: 2.09 us -> 1.27 us  [packed_fields(): pl.pallas_call(functools.partial(pack_kernel, rows, cols), out_shape=(jax...]
    ppermute x11, starting transfers between devices: 14.1 us -> 14.9 us  [moved(): return lax.ppermute(value, ('lat', 'lon'), pairs)]
    unnamed x3 -> x2, local copies, waits for them, and re-layouts: 0.73 us -> 0.01 us
    reshape x1, local copies, waits for them, and re-layouts: 0.1 us -> 0.71 us  [shards(): adjoint_state = jnp.swapaxes(adjoint.reshape(2, levels, cols, rows), 2, 3)]
  transfers between devices with their start and end apart: 11 -> 11, of which waited for: 8 -> 6; matrix products, arithmetic and copies ran while one was open for 4% -> 4% of each run, Pallas kernels for 10% -> 8%
where the time goes in v5:
time: 26.6 us; the launch traced here: 26.5 us
  starting transfers between devices  14.9 us (56%)
  waiting for transfers between devices  6.88 us (26%)
  Pallas kernels  2.81 us (11%)
  local copies, waits for them, and re-layouts  0.72 us (3%)
  between operations  0.69 us (3%)
  matrix products  0.51 us (2%)
    ppermute x11, starting transfers between devices, moved(): return lax.ppermute(value, ('lat', 'lon'), pairs)  14.9 us
    ppermute x11, waiting for transfers between devices, moved(): return lax.ppermute(value, ('lat', 'lon'), pairs)  6.88 us
    pallas_call x1, Pallas kernels, packed_fields(): pl.pallas_call(functools.partial(pack_kernel, rows, cols), out_shape=(jax...  1.27 us
    pallas_call x1, Pallas kernels, band_vectors(): pl.pallas_call(functools.partial(band_kernel, rows, cols, blocks, exchang...  0.91 us
    reshape x1, local copies, waits for them, and re-layouts, shards(): adjoint_state = jnp.swapaxes(adjoint.reshape(2, levels, cols, rows), 2, 3)  0.71 us
    pallas_call x1, Pallas kernels, scattered(): pl.pallas_call(sum_kernel, out_shape=[jax.ShapeDtypeStruct(shape, jnp.flo...  0.63 us
  transfers between devices with their start and end apart: 11, of which 6 were waited for; matrix products, arithmetic and copies ran while one was open for 4% of the time, Pallas kernels for 8%

profile of v5, /device:TPU:0, one launch (start us, length us, event | category | flops | bytes accessed | tf_op | source)
XLA Modules:
  0.0 26.5 jit_solution(8999732318733125655)
XLA Ops:
  0.6 0.0 copy-start
  0.6 0.6 %collective-permute-start.7 = (bf16[1024,4,128]{2,1,0:T(4,128)(2,1)}, bf16[1024,4,128]{2,1,0:T(4,128)(2,1)S(1)}, u32[]{:S(2)}, u32[]{:S(2)}) collective-permute-start(bf16[1024,4,128]{2,1,0:T(4,128)(2,1)} %param.9), channel_id=1, source_target_pairs={{0,1},{1,0},{2,3},{3,2},{4,5},{5,4},{6,7},{7,6},{8,9},{9,8},{10,11... | collective-permute-start | bytes 3145736 | tf_op jit(solution)/shard_map/ppermute | solution.py:214
  1.2 1.3 %pack.1 = (f32[56,128]{1,0:T(8,128)S(1)}, f32[16,128]{1,0:T(8,128)S(1)}, f32[16,128]{1,0:T(8,128)S(1)}) custom-call(f32[256,16]{1,0:T(8,128)} %bitcast.32, f32[64,16]{1,0:T(8,128)} %bitcast.36, f32[64,16]{1,0:T(8,128)} %bitcast.37, f32[56,16]{1,0:T(8,128)} %bitcast.38), custom_call_target="tpu_custom_call" | custom-call | tf_op jit(solution)/shard_map/pack/pallas_call | solution.py:75
  2.5 2.7 %collective-permute-start = (f32[16,128]{1,0:T(8,128)S(1)}, f32[16,128]{1,0:T(8,128)S(1)}, u32[]{:S(2)}, u32[]{:S(2)}) collective-permute-start(f32[16,128]{1,0:T(8,128)S(1)} %get-tuple-element.11), channel_id=1, source_target_pairs={{0,9},{1,8},{2,11},{3,10},{4,13},{5,12},{6,15},{7,14},{8,1},{9,0},... | collective-permute-start | bytes 24584 | tf_op jit(solution)/shard_map/ppermute | solution.py:214
  5.1 1.2 %collective-permute-start.1 = (f32[16,128]{1,0:T(8,128)S(1)}, f32[16,128]{1,0:T(8,128)S(1)}, u32[]{:S(2)}, u32[]{:S(2)}) collective-permute-start(f32[16,128]{1,0:T(8,128)S(1)} %get-tuple-element.12), channel_id=1, source_target_pairs={{0,25},{1,24},{2,27},{3,26},{4,29},{5,28},{6,31},{7,30},{8,17},{9,... | collective-permute-start | bytes 24584 | tf_op jit(solution)/shard_map/ppermute | solution.py:214
  6.3 2.6 %collective-permute-start.3 = (f32[56,128]{1,0:T(8,128)S(1)}, f32[56,128]{1,0:T(8,128)S(1)}, u32[]{:S(2)}, u32[]{:S(2)}) collective-permute-start(f32[56,128]{1,0:T(8,128)S(1)} %get-tuple-element.10), channel_id=1, source_target_pairs={{0,5},{1,4},{2,7},{3,6},{4,1},{5,0},{6,3},{7,2},{8,13},{9,12},{10,... | collective-permute-start | bytes 86024 | tf_op jit(solution)/shard_map/ppermute | solution.py:214
  8.9 0.0 collective-permute-done
  8.9 0.2 collective-permute-done.1
  9.1 2.3 %collective-permute-start.4 = (f32[16,128]{1,0:T(8,128)S(1)}, f32[16,128]{1,0:T(8,128)S(1)}, u32[]{:S(2)}, u32[]{:S(2)}) collective-permute-start(f32[16,128]{1,0:T(8,128)S(1)} %add.15), channel_id=1, source_target_pairs={{0,5},{1,4},{2,7},{3,6},{4,1},{5,0},{6,3},{7,2},{8,13},{9,12},{10,... | collective-permute-start | bytes 24584 | tf_op jit(solution)/shard_map/ppermute | solution.py:214
  11.4 1.3 %collective-permute-start.5 = (f32[72,128]{1,0:T(8,128)S(1)}, f32[72,128]{1,0:T(8,128)S(1)}, u32[]{:S(2)}, u32[]{:S(2)}) collective-permute-start(f32[72,128]{1,0:T(8,128)S(1)} %get-tuple-element.21), channel_id=1, source_target_pairs={{0,7},{1,6},{2,5},{3,4},{4,3},{5,2},{6,1},{7,0},{8,15},{9,14},{10,... | collective-permute-start | bytes 110600 | tf_op jit(solution)/shard_map/ppermute | solution.py:214
  12.8 0.3 %collective-permute-start.2 = (f32[72,128]{1,0:T(8,128)S(1)}, f32[72,128]{1,0:T(8,128)S(1)}, u32[]{:S(2)}, u32[]{:S(2)}) collective-permute-start(f32[72,128]{1,0:T(8,128)S(1)} %get-tuple-element.21), channel_id=1, source_target_pairs={{0,3},{1,2},{2,1},{3,0},{4,7},{5,6},{6,5},{7,4},{8,11},{9,10},{10,... | collective-permute-start | bytes 110600 | tf_op jit(solution)/shard_map/ppermute | solution.py:214
  13.1 0.0 collective-permute-done.4
  13.1 0.0 collective-permute-done.3
  13.1 3.6 %collective-permute-done.5 = f32[72,128]{1,0:T(8,128)S(1)} collective-permute-done((f32[72,128]{1,0:T(8,128)S(1)}, f32[72,128]{1,0:T(8,128)S(1)}, u32[]{:S(2)}, u32[]{:S(2)}) %collective-permute-start.5) | collective-permute-done | bytes 36896 | tf_op jit(solution)/shard_map/ppermute | solution.py:214
  16.7 0.0 collective-permute-done.2
  16.7 0.6 %collective-permute-start.6 = (f32[4,72,128]{2,1,0:T(8,128)S(1)}, f32[4,72,128]{2,1,0:T(8,128)S(1)}, u32[]{:S(2)}, u32[]{:S(2)}) collective-permute-start(f32[4,72,128]{2,1,0:T(8,128)S(1)} %pad_maximum_fusion.refs_0_), channel_id=1, source_target_pairs={{0,1},{1,0},{2,3},{3,2},{4,5},{5,4},{6,7},{7,6},{8,9},{9,8},{10,11... | collective-permute-start | bytes 442376 | tf_op jit(solution)/shard_map/ppermute | solution.py:214
  17.4 1.0 %collective-permute-done.6.refs_1_ = f32[4,72,128]{2,1,0:T(8,128)S(1)} collective-permute-done((f32[4,72,128]{2,1,0:T(8,128)S(1)}, f32[4,72,128]{2,1,0:T(8,128)S(1)}, u32[]{:S(2)}, u32[]{:S(2)}) %collective-permute-start.6) | collective-permute-done | bytes 147488 | tf_op jit(solution)/shard_map/ppermute | solution.py:214
  18.4 0.9 %band.1 = (bf16[18,1024]{1,0:T(8,128)(2,1)S(1)}, f32[16,128]{1,0:T(8,128)S(1)}) custom-call(f32[4,72,128]{2,1,0:T(8,128)S(1)} %pad_maximum_fusion.refs_0_, f32[4,72,128]{2,1,0:T(8,128)S(1)} %collective-permute-done.6.refs_1_), custom_call_target="tpu_custom_call" | custom-call | tf_op jit(solution)/shard_map/band/pallas_call | solution.py:196
  19.3 0.0 copy-done
  19.3 0.3 fusion.2
  19.6 0.0 collective-permute-done.7
  19.6 0.3 fusion
  19.8 1.5 %collective-permute-start.10 = (f32[1,18,128]{2,1,0:T(8,128)S(1)}, f32[1,18,128]{2,1,0:T(8,128)S(1)}, u32[]{:S(2)}, u32[]{:S(2)}) collective-permute-start(f32[1,18,128]{2,1,0:T(8,128)S(1)} %get-tuple-element.17), channel_id=1, source_target_pairs={{0,25},{1,24},{2,27},{3,26},{4,29},{5,28},{6,31},{7,30},{8,17},{9,... | collective-permute-start | bytes 27656 | tf_op jit(solution)/shard_map/ppermute | solution.py:214
  21.4 1.4 %collective-permute-start.8 = (f32[1,18,128]{2,1,0:T(8,128)S(1)}, f32[1,18,128]{2,1,0:T(8,128)S(1)}, u32[]{:S(2)}, u32[]{:S(2)}) collective-permute-start(f32[1,18,128]{2,1,0:T(8,128)S(1)} %get-tuple-element.19), channel_id=1, source_target_pairs={{0,9},{1,8},{2,11},{3,10},{4,13},{5,12},{6,15},{7,14},{8,1},{9,0},... | collective-permute-start | bytes 27656 | tf_op jit(solution)/shard_map/ppermute | solution.py:214
  22.7 0.3 %collective-permute-start.9 = (f32[1,18,128]{2,1,0:T(8,128)S(1)}, f32[1,18,128]{2,1,0:T(8,128)S(1)}, u32[]{:S(2)}, u32[]{:S(2)}) collective-permute-start(f32[1,18,128]{2,1,0:T(8,128)S(1)} %get-tuple-element.18), channel_id=1, source_target_pairs={{0,17},{1,16},{2,19},{3,18},{4,21},{5,20},{6,23},{7,22},{8,25},{9,... | collective-permute-start | bytes 27656 | tf_op jit(solution)/shard_map/ppermute | solution.py:214
  23.1 0.7 %reshape.29 = f32[2,8,8,16]{3,2,1,0:T(8,128)} reshape(f32[16,128]{1,0:T(8,128)S(1)} %get-tuple-element.13) | data formatting | bytes 16384 | tf_op jit(solution)/shard_map/reshape | solution.py:294
  23.8 0.1 collective-permute-done.10.refs_2_
  23.9 0.6 %collective-permute-done.8.refs_0_ = f32[1,18,128]{2,1,0:T(8,128)S(1)} collective-permute-done((f32[1,18,128]{2,1,0:T(8,128)S(1)}, f32[1,18,128]{2,1,0:T(8,128)S(1)}, u32[]{:S(2)}, u32[]{:S(2)}) %collective-permute-start.8) | collective-permute-done | bytes 9248 | tf_op jit(solution)/shard_map/ppermute | solution.py:214
  24.5 1.4 %collective-permute-done.9.refs_1_ = f32[1,18,128]{2,1,0:T(8,128)S(1)} collective-permute-done((f32[1,18,128]{2,1,0:T(8,128)S(1)}, f32[1,18,128]{2,1,0:T(8,128)S(1)}, u32[]{:S(2)}, u32[]{:S(2)}) %collective-permute-start.9) | collective-permute-done | bytes 9248 | tf_op jit(solution)/shard_map/ppermute | solution.py:214
  25.9 0.6 %total.1 = (f32[2,8,1,128]{3,2,1,0:T(1,128)}, f32[2,1,128]{2,1,0:T(1,128)}) custom-call(f32[1,18,128]{2,1,0:T(8,128)S(1)} %dynamic-slice_bitcast_fusion.3.own_ref, f32[1,18,128]{2,1,0:T(8,128)S(1)} %collective-permute-done.8.refs_0_, f32[1,18,128]{2,1,0:T(8,128)S(1)} %collective-permute-done.9.refs_1_, f32[1,18,128]{2,1,0:T(8,128)S(1)} %collective-permute-done.10.refs_2_), custom_call_target="tpu_custom_call" | custom-call | tf_op jit(solution)/shard_map/total/pallas_call | solution.py:273
  (6 shorter events, 0.0 us)
Async XLA Ops:
  0.6 18.7 %copy-start = (bf16[1024,4,128]{2,1,0:T(4,128)(2,1)S(1)}, bf16[1024,4,128]{2,1,0:T(4,128)(2,1)}, u32[]{:S(2)}) copy-start(bf16[1024,4,128]{2,1,0:T(4,128)(2,1)} %param.9) | copy-start | bytes 3145732
  0.6 18.9 %collective-permute-start.7 = (bf16[1024,4,128]{2,1,0:T(4,128)(2,1)}, bf16[1024,4,128]{2,1,0:T(4,128)(2,1)S(1)}, u32[]{:S(2)}, u32[]{:S(2)}) collective-permute-start(bf16[1024,4,128]{2,1,0:T(4,128)(2,1)} %param.9), channel_id=1, source_target_pairs={{0,1},{1,0},{2,3},{3,2},{4,5},{5,4},{6,7},{7,6},{8,9},{9,8},{10,11... | collective-permute-start | bytes 3145736 | tf_op jit(solution)/shard_map/ppermute | solution.py:214
  2.5 6.5 %collective-permute-start = (f32[16,128]{1,0:T(8,128)S(1)}, f32[16,128]{1,0:T(8,128)S(1)}, u32[]{:S(2)}, u32[]{:S(2)}) collective-permute-start(f32[16,128]{1,0:T(8,128)S(1)} %get-tuple-element.11), channel_id=1, source_target_pairs={{0,9},{1,8},{2,11},{3,10},{4,13},{5,12},{6,15},{7,14},{8,1},{9,0},... | collective-permute-start | bytes 24584 | tf_op jit(solution)/shard_map/ppermute | solution.py:214
  5.1 4.0 %collective-permute-start.1 = (f32[16,128]{1,0:T(8,128)S(1)}, f32[16,128]{1,0:T(8,128)S(1)}, u32[]{:S(2)}, u32[]{:S(2)}) collective-permute-start(f32[16,128]{1,0:T(8,128)S(1)} %get-tuple-element.12), channel_id=1, source_target_pairs={{0,25},{1,24},{2,27},{3,26},{4,29},{5,28},{6,31},{7,30},{8,17},{9,... | collective-permute-start | bytes 24584 | tf_op jit(solution)/shard_map/ppermute | solution.py:214
  6.3 6.8 %collective-permute-start.3 = (f32[56,128]{1,0:T(8,128)S(1)}, f32[56,128]{1,0:T(8,128)S(1)}, u32[]{:S(2)}, u32[]{:S(2)}) collective-permute-start(f32[56,128]{1,0:T(8,128)S(1)} %get-tuple-element.10), channel_id=1, source_target_pairs={{0,5},{1,4},{2,7},{3,6},{4,1},{5,0},{6,3},{7,2},{8,13},{9,12},{10,... | collective-permute-start | bytes 86024 | tf_op jit(solution)/shard_map/ppermute | solution.py:214
  9.1 4.0 %collective-permute-start.4 = (f32[16,128]{1,0:T(8,128)S(1)}, f32[16,128]{1,0:T(8,128)S(1)}, u32[]{:S(2)}, u32[]{:S(2)}) collective-permute-start(f32[16,128]{1,0:T(8,128)S(1)} %add.15), channel_id=1, source_target_pairs={{0,5},{1,4},{2,7},{3,6},{4,1},{5,0},{6,3},{7,2},{8,13},{9,12},{10,... | collective-permute-start | bytes 24584 | tf_op jit(solution)/shard_map/ppermute | solution.py:214
  11.4 5.3 %collective-permute-start.5 = (f32[72,128]{1,0:T(8,128)S(1)}, f32[72,128]{1,0:T(8,128)S(1)}, u32[]{:S(2)}, u32[]{:S(2)}) collective-permute-start(f32[72,128]{1,0:T(8,128)S(1)} %get-tuple-element.21), channel_id=1, source_target_pairs={{0,7},{1,6},{2,5},{3,4},{4,3},{5,2},{6,1},{7,0},{8,15},{9,14},{10,... | collective-permute-start | bytes 110600 | tf_op jit(solution)/shard_map/ppermute | solution.py:214
  12.8 3.9 %collective-permute-start.2 = (f32[72,128]{1,0:T(8,128)S(1)}, f32[72,128]{1,0:T(8,128)S(1)}, u32[]{:S(2)}, u32[]{:S(2)}) collective-permute-start(f32[72,128]{1,0:T(8,128)S(1)} %get-tuple-element.21), channel_id=1, source_target_pairs={{0,3},{1,2},{2,1},{3,0},{4,7},{5,6},{6,5},{7,4},{8,11},{9,10},{10,... | collective-permute-start | bytes 110600 | tf_op jit(solution)/shard_map/ppermute | solution.py:214
  16.7 1.7 %collective-permute-start.6 = (f32[4,72,128]{2,1,0:T(8,128)S(1)}, f32[4,72,128]{2,1,0:T(8,128)S(1)}, u32[]{:S(2)}, u32[]{:S(2)}) collective-permute-start(f32[4,72,128]{2,1,0:T(8,128)S(1)} %pad_maximum_fusion.refs_0_), channel_id=1, source_target_pairs={{0,1},{1,0},{2,3},{3,2},{4,5},{5,4},{6,7},{7,6},{8,9},{9,8},{10,11... | collective-permute-start | bytes 442376 | tf_op jit(solution)/shard_map/ppermute | solution.py:214
  19.8 4.1 %collective-permute-start.10 = (f32[1,18,128]{2,1,0:T(8,128)S(1)}, f32[1,18,128]{2,1,0:T(8,128)S(1)}, u32[]{:S(2)}, u32[]{:S(2)}) collective-permute-start(f32[1,18,128]{2,1,0:T(8,128)S(1)} %get-tuple-element.17), channel_id=1, source_target_pairs={{0,25},{1,24},{2,27},{3,26},{4,29},{5,28},{6,31},{7,30},{8,17},{9,... | collective-permute-start | bytes 27656 | tf_op jit(solution)/shard_map/ppermute | solution.py:214
  21.4 3.1 %collective-permute-start.8 = (f32[1,18,128]{2,1,0:T(8,128)S(1)}, f32[1,18,128]{2,1,0:T(8,128)S(1)}, u32[]{:S(2)}, u32[]{:S(2)}) collective-permute-start(f32[1,18,128]{2,1,0:T(8,128)S(1)} %get-tuple-element.19), channel_id=1, source_target_pairs={{0,9},{1,8},{2,11},{3,10},{4,13},{5,12},{6,15},{7,14},{8,1},{9,0},... | collective-permute-start | bytes 27656 | tf_op jit(solution)/shard_map/ppermute | solution.py:214
  22.7 3.1 %collective-permute-start.9 = (f32[1,18,128]{2,1,0:T(8,128)S(1)}, f32[1,18,128]{2,1,0:T(8,128)S(1)}, u32[]{:S(2)}, u32[]{:S(2)}) collective-permute-start(f32[1,18,128]{2,1,0:T(8,128)S(1)} %get-tuple-element.18), channel_id=1, source_target_pairs={{0,17},{1,16},{2,19},{3,18},{4,21},{5,20},{6,23},{7,22},{8,25},{9,... | collective-permute-start | bytes 27656 | tf_op jit(solution)/shard_map/ppermute | solution.py:214

commit v6 on v5

--- a/solution.py
+++ b/solution.py
@@ -24,7 +24,7 @@
                 forcing_ref, zonal_ref, merid_ref, mixing_ref, sems):
     levels = zonal_hbm.shape[0] // cols
     copies = [
-        pltpu.make_async_copy(source, target, sems.at[i])
+        pltpu.make_async_copy(source, target.at[pl.ds(0, source.shape[0])], sems.at[i])
         for i, (source, target) in enumerate(
             ((forcing_hbm, forcing_ref), (zonal_hbm, zonal_ref), (merid_hbm, merid_ref), (mixing_hbm, mixing_ref)))
     ]
@@ -77,7 +77,7 @@
         out_shape=(jax.ShapeDtypeStruct((56, cells), jnp.float32), edge, edge),
         in_specs=[pl.BlockSpec(memory_space=pltpu.HBM)] * 4,
         out_specs=[pl.BlockSpec(memory_space=pltpu.VMEM)] * 3,
-        scratch_shapes=[pltpu.VMEM(v.shape, jnp.float32) for v in fields] + [pltpu.SemaphoreType.DMA((4,))],
+        scratch_shapes=[pltpu.VMEM((v.shape[0] + 2 * cols, rows), jnp.float32) for v in fields] + [pltpu.SemaphoreType.DMA((4,))],
         compiler_params=pltpu.CompilerParams(vmem_limit_bytes=GRANT),
         name="pack",
     )(*values)
@@ -147,7 +147,7 @@
 
     def diffuse(value, mix):
         flow = mix * (roll(value, -1, -2) - value)
-        return value + flow - roll(flow, 1, -2)
+        return value + flow - roll(mix, 1, -2) * (value - roll(value, 1, -2))
 
     def factors(across, along, edge=None):
         out_east = jnp.maximum(across, 0.0)
@@ -215,7 +215,9 @@
 
 
 def along_lat(nearer, farther):
-    farther = moved(farther, lambda lat, lon: (lat + 1 if lat % 2 else lat - 1, lon ^ EDGE_CROSS))
+    ends = (0, lax.axis_size("lat") - 1)
+    farther = moved(farther, lambda lat, lon: (
+        (lat, lon ^ 1) if lat in ends else (lat + 1 if lat % 2 else lat - 1, lon ^ EDGE_CROSS)))
     nearer = moved(nearer, lambda lat, lon: (lat ^ 1, lon ^ EDGE_CROSS))
     return nearer + farther
 
@@ -225,17 +227,20 @@
     packed = jnp.concatenate([main, halo], 0)
     if peers > 2 * DIRECT:
         return (lax.all_gather(packed, "lon", axis=0),), False
-    pieces = [packed]
+    pieces = {}
     for apart in range(2, peers, 2):
         target = lambda lat, lon: (lat, lon ^ apart ^ CHIP_CROSS)
         if apart in EARLY:
             ahead = moved(main, target)
             behind = moved(halo, target)
-            pieces.append(jnp.concatenate([ahead, behind], 0))
+            pieces[apart] = jnp.concatenate([ahead, behind], 0)
         else:
-            pieces.append(moved(packed, target))
-    same = jnp.stack(pieces)
-    return (same, moved(same, lambda lat, lon: (lat, lon ^ 1))), True
+            pieces[apart] = moved(packed, target)
+    also = moved(packed, lambda lat, lon: (lat, lon ^ 2 ^ 1 ^ CHIP_CROSS))
+    far = [pieces[apart] for apart in range(4, peers, 2)]
+    swapped = moved(jnp.stack([packed] + far), lambda lat, lon: (lat, lon ^ 1))
+    same = jnp.stack([packed, pieces[2]] + far)
+    return (same, jnp.concatenate([swapped[:1], also[None], swapped[1:]], 0)), True
 
 
 def sum_kernel(own_ref, *refs):

time: 26.6 us -> 26.3 us (0.989)
  waiting for transfers between devices: 6.88 us -> 4.96 us
  starting transfers between devices: 14.9 us -> 16.4 us
    ppermute x11 -> x12, waiting for transfers between devices: 6.88 us -> 4.96 us  [moved(): return lax.ppermute(value, ('lat', 'lon'), pairs)]
    ppermute x11 -> x12, starting transfers between devices: 14.9 us -> 16.4 us  [moved(): return lax.ppermute(value, ('lat', 'lon'), pairs)]
  transfers between devices with their start and end apart: 11 -> 12, of which waited for: 6 -> 4; matrix products, arithmetic and copies ran while one was open for 4% -> 4% of each run, Pallas kernels for 8% -> 8%
where the time goes in v6:
time: 26.3 us; the launch traced here: 26.2 us
  starting transfers between devices  16.4 us (62%)
  waiting for transfers between devices  4.96 us (19%)
  Pallas kernels  2.83 us (11%)
  local copies, waits for them, and re-layouts  0.74 us (3%)
  between operations  0.73 us (3%)
  matrix products  0.51 us (2%)
    ppermute x12, starting transfers between devices, moved(): return lax.ppermute(value, ('lat', 'lon'), pairs)  16.4 us
    ppermute x12, waiting for transfers between devices, moved(): return lax.ppermute(value, ('lat', 'lon'), pairs)  4.96 us
    pallas_call x1, Pallas kernels, packed_fields(): pl.pallas_call(functools.partial(pack_kernel, rows, cols), out_shape=(jax...  1.27 us
    pallas_call x1, Pallas kernels, band_vectors(): pl.pallas_call(functools.partial(band_kernel, rows, cols, blocks, exchang...  0.93 us
    reshape x1, local copies, waits for them, and re-layouts, shards(): adjoint_state = jnp.swapaxes(adjoint.reshape(2, levels, cols, rows), 2, 3)  0.71 us
    pallas_call x1, Pallas kernels, scattered(): pl.pallas_call(sum_kernel, out_shape=[jax.ShapeDtypeStruct(shape, jnp.flo...  0.63 us
  transfers between devices with their start and end apart: 12, of which 4 were waited for; matrix products, arithmetic and copies ran while one was open for 4% of the time, Pallas kernels for 8%

profile of v6, /device:TPU:0, one launch (start us, length us, event | category | flops | bytes accessed | tf_op | source)
XLA Modules:
  0.0 26.2 jit_solution(17651682677539369465)
XLA Ops:
  0.6 0.0 copy-start
  0.6 0.6 %collective-permute-start.8 = (bf16[1024,4,128]{2,1,0:T(4,128)(2,1)}, bf16[1024,4,128]{2,1,0:T(4,128)(2,1)S(1)}, u32[]{:S(2)}, u32[]{:S(2)}) collective-permute-start(bf16[1024,4,128]{2,1,0:T(4,128)(2,1)} %param.9), channel_id=1, source_target_pairs={{0,1},{1,0},{2,3},{3,2},{4,5},{5,4},{6,7},{7,6},{8,9},{9,8},{10,11... | collective-permute-start | bytes 3145736 | tf_op jit(solution)/shard_map/ppermute | solution.py:214
  1.2 1.3 %pack.1 = (f32[56,128]{1,0:T(8,128)S(1)}, f32[16,128]{1,0:T(8,128)S(1)}, f32[16,128]{1,0:T(8,128)S(1)}) custom-call(f32[256,16]{1,0:T(8,128)} %bitcast.35, f32[64,16]{1,0:T(8,128)} %bitcast.39, f32[64,16]{1,0:T(8,128)} %bitcast.40, f32[56,16]{1,0:T(8,128)} %bitcast.41), custom_call_target="tpu_custom_call" | custom-call | tf_op jit(solution)/shard_map/pack/pallas_call | solution.py:75
  2.5 2.7 %collective-permute-start = (f32[16,128]{1,0:T(8,128)S(1)}, f32[16,128]{1,0:T(8,128)S(1)}, u32[]{:S(2)}, u32[]{:S(2)}) collective-permute-start(f32[16,128]{1,0:T(8,128)S(1)} %get-tuple-element.11), channel_id=1, source_target_pairs={{0,9},{1,8},{2,11},{3,10},{4,13},{5,12},{6,15},{7,14},{8,1},{9,0},... | collective-permute-start | bytes 24584 | tf_op jit(solution)/shard_map/ppermute | solution.py:214
  5.1 0.1 collective-permute-start.1
  5.2 2.6 %collective-permute-start.3 = (f32[56,128]{1,0:T(8,128)S(1)}, f32[56,128]{1,0:T(8,128)S(1)}, u32[]{:S(2)}, u32[]{:S(2)}) collective-permute-start(f32[56,128]{1,0:T(8,128)S(1)} %get-tuple-element.10), channel_id=1, source_target_pairs={{0,5},{1,4},{2,7},{3,6},{4,1},{5,0},{6,3},{7,2},{8,13},{9,12},{10,... | collective-permute-start | bytes 86024 | tf_op jit(solution)/shard_map/ppermute | solution.py:214
  7.8 0.0 collective-permute-done
  7.8 0.0 collective-permute-done.1
  7.9 1.5 %collective-permute-start.4 = (f32[16,128]{1,0:T(8,128)S(1)}, f32[16,128]{1,0:T(8,128)S(1)}, u32[]{:S(2)}, u32[]{:S(2)}) collective-permute-start(f32[16,128]{1,0:T(8,128)S(1)} %add.15), channel_id=1, source_target_pairs={{0,5},{1,4},{2,7},{3,6},{4,1},{5,0},{6,3},{7,2},{8,13},{9,12},{10,... | collective-permute-start | bytes 24584 | tf_op jit(solution)/shard_map/ppermute | solution.py:214
  9.3 2.3 %collective-permute-start.5 = (f32[72,128]{1,0:T(8,128)S(1)}, f32[72,128]{1,0:T(8,128)S(1)}, u32[]{:S(2)}, u32[]{:S(2)}) collective-permute-start(f32[72,128]{1,0:T(8,128)S(1)} %get-tuple-element.21), channel_id=1, source_target_pairs={{0,7},{1,6},{2,5},{3,4},{4,3},{5,2},{6,1},{7,0},{8,15},{9,14},{10,... | collective-permute-start | bytes 110600 | tf_op jit(solution)/shard_map/ppermute | solution.py:214
  11.6 0.0 collective-permute-start.7
  11.6 0.3 %collective-permute-done.4 = f32[16,128]{1,0:T(8,128)S(1)} collective-permute-done((f32[16,128]{1,0:T(8,128)S(1)}, f32[16,128]{1,0:T(8,128)S(1)}, u32[]{:S(2)}, u32[]{:S(2)}) %collective-permute-start.4) | collective-permute-done | bytes 8224 | tf_op jit(solution)/shard_map/ppermute | solution.py:214
  11.9 1.3 %collective-permute-start.2 = (f32[72,128]{1,0:T(8,128)S(1)}, f32[72,128]{1,0:T(8,128)S(1)}, u32[]{:S(2)}, u32[]{:S(2)}) collective-permute-start(f32[72,128]{1,0:T(8,128)S(1)} %get-tuple-element.21), channel_id=1, source_target_pairs={{0,3},{1,2},{2,1},{3,0},{4,7},{5,6},{6,5},{7,4},{8,11},{9,10},{10,... | collective-permute-start | bytes 110600 | tf_op jit(solution)/shard_map/ppermute | solution.py:214
  13.2 0.0 collective-permute-done.3
  13.2 1.5 %collective-permute-done.5 = f32[72,128]{1,0:T(8,128)S(1)} collective-permute-done((f32[72,128]{1,0:T(8,128)S(1)}, f32[72,128]{1,0:T(8,128)S(1)}, u32[]{:S(2)}, u32[]{:S(2)}) %collective-permute-start.5) | collective-permute-done | bytes 36896 | tf_op jit(solution)/shard_map/ppermute | solution.py:214
  14.7 0.4 %collective-permute-start.6 = (f32[3,72,128]{2,1,0:T(8,128)S(1)}, f32[3,72,128]{2,1,0:T(8,128)S(1)}, u32[]{:S(2)}, u32[]{:S(2)}) collective-permute-start(f32[3,72,128]{2,1,0:T(8,128)S(1)} %pad_maximum_fusion.2), channel_id=1, source_target_pairs={{0,1},{1,0},{2,3},{3,2},{4,5},{5,4},{6,7},{7,6},{8,9},{9,8},{10,11... | collective-permute-start | bytes 331784 | tf_op jit(solution)/shard_map/ppermute | solution.py:214
  15.1 1.2 %collective-permute-done.2 = f32[72,128]{1,0:T(8,128)S(1)} collective-permute-done((f32[72,128]{1,0:T(8,128)S(1)}, f32[72,128]{1,0:T(8,128)S(1)}, u32[]{:S(2)}, u32[]{:S(2)}) %collective-permute-start.2) | collective-permute-done | bytes 36896 | tf_op jit(solution)/shard_map/ppermute | solution.py:214
  16.2 0.0 collective-permute-done.6
  16.3 0.0 collective-permute-done.7
  16.3 0.9 %band.1 = (bf16[18,1024]{1,0:T(8,128)(2,1)S(1)}, f32[16,128]{1,0:T(8,128)S(1)}) custom-call(f32[4,72,128]{2,1,0:T(8,128)S(1)} %pad_maximum_fusion.refs_0_, f32[4,72,128]{2,1,0:T(8,128)S(1)} %pad_maximum_fusion.1.refs_1_), custom_call_target="tpu_custom_call" | custom-call | tf_op jit(solution)/shard_map/band/pallas_call | solution.py:196
  17.3 0.0 copy-done
  17.3 0.3 fusion.2
  17.5 0.0 collective-permute-done.8
  17.5 0.3 fusion
  17.8 3.7 %collective-permute-start.10 = (f32[1,18,128]{2,1,0:T(8,128)S(1)}, f32[1,18,128]{2,1,0:T(8,128)S(1)}, u32[]{:S(2)}, u32[]{:S(2)}) collective-permute-start(f32[1,18,128]{2,1,0:T(8,128)S(1)} %get-tuple-element.18), channel_id=1, source_target_pairs={{0,17},{1,16},{2,19},{3,18},{4,21},{5,20},{6,23},{7,22},{8,25},{9,... | collective-permute-start | bytes 27656 | tf_op jit(solution)/shard_map/ppermute | solution.py:214
  21.5 0.2 collective-permute-start.11
  21.7 1.1 %collective-permute-start.9 = (f32[1,18,128]{2,1,0:T(8,128)S(1)}, f32[1,18,128]{2,1,0:T(8,128)S(1)}, u32[]{:S(2)}, u32[]{:S(2)}) collective-permute-start(f32[1,18,128]{2,1,0:T(8,128)S(1)} %get-tuple-element.19), channel_id=1, source_target_pairs={{0,9},{1,8},{2,11},{3,10},{4,13},{5,12},{6,15},{7,14},{8,1},{9,0},... | collective-permute-start | bytes 27656 | tf_op jit(solution)/shard_map/ppermute | solution.py:214
  22.8 0.7 %reshape.29 = f32[2,8,8,16]{3,2,1,0:T(8,128)} reshape(f32[16,128]{1,0:T(8,128)S(1)} %get-tuple-element.13) | data formatting | bytes 16384 | tf_op jit(solution)/shard_map/reshape | solution.py:299
  23.5 0.0 collective-permute-done.10.refs_1_
  23.5 2.0 %collective-permute-done.11.refs_2_ = f32[1,18,128]{2,1,0:T(8,128)S(1)} collective-permute-done((f32[1,18,128]{2,1,0:T(8,128)S(1)}, f32[1,18,128]{2,1,0:T(8,128)S(1)}, u32[]{:S(2)}, u32[]{:S(2)}) %collective-permute-start.11) | collective-permute-done | bytes 9248 | tf_op jit(solution)/shard_map/ppermute | solution.py:214
  25.5 0.0 collective-permute-done.9.refs_0_
  25.5 0.6 %total.1 = (f32[2,8,1,128]{3,2,1,0:T(1,128)}, f32[2,1,128]{2,1,0:T(1,128)}) custom-call(f32[1,18,128]{2,1,0:T(8,128)S(1)} %dynamic-slice_bitcast_fusion.3.own_ref, f32[1,18,128]{2,1,0:T(8,128)S(1)} %collective-permute-done.9.refs_0_, f32[1,18,128]{2,1,0:T(8,128)S(1)} %collective-permute-done.10.refs_1_, f32[1,18,128]{2,1,0:T(8,128)S(1)} %collective-permute-done.11.refs_2_), custom_call_target="tpu_custom_call" | custom-call | tf_op jit(solution)/shard_map/total/pallas_call | solution.py:278
  (10 shorter events, 0.1 us)
Async XLA Ops:
  0.6 16.6 %copy-start = (bf16[1024,4,128]{2,1,0:T(4,128)(2,1)S(1)}, bf16[1024,4,128]{2,1,0:T(4,128)(2,1)}, u32[]{:S(2)}) copy-start(bf16[1024,4,128]{2,1,0:T(4,128)(2,1)} %param.9) | copy-start | bytes 3145732
  0.6 16.9 %collective-permute-start.8 = (bf16[1024,4,128]{2,1,0:T(4,128)(2,1)}, bf16[1024,4,128]{2,1,0:T(4,128)(2,1)S(1)}, u32[]{:S(2)}, u32[]{:S(2)}) collective-permute-start(bf16[1024,4,128]{2,1,0:T(4,128)(2,1)} %param.9), channel_id=1, source_target_pairs={{0,1},{1,0},{2,3},{3,2},{4,5},{5,4},{6,7},{7,6},{8,9},{9,8},{10,11... | collective-permute-start | bytes 3145736 | tf_op jit(solution)/shard_map/ppermute | solution.py:214
  2.5 5.4 %collective-permute-start = (f32[16,128]{1,0:T(8,128)S(1)}, f32[16,128]{1,0:T(8,128)S(1)}, u32[]{:S(2)}, u32[]{:S(2)}) collective-permute-start(f32[16,128]{1,0:T(8,128)S(1)} %get-tuple-element.11), channel_id=1, source_target_pairs={{0,9},{1,8},{2,11},{3,10},{4,13},{5,12},{6,15},{7,14},{8,1},{9,0},... | collective-permute-start | bytes 24584 | tf_op jit(solution)/shard_map/ppermute | solution.py:214
  5.1 2.7 %collective-permute-start.1 = (f32[16,128]{1,0:T(8,128)S(1)}, f32[16,128]{1,0:T(8,128)S(1)}, u32[]{:S(2)}, u32[]{:S(2)}) collective-permute-start(f32[16,128]{1,0:T(8,128)S(1)} %get-tuple-element.12), channel_id=1, source_target_pairs={{0,1},{1,0},{2,3},{3,2},{4,5},{5,4},{6,7},{7,6},{8,17},{9,16},{10,... | collective-permute-start | bytes 24584 | tf_op jit(solution)/shard_map/ppermute | solution.py:214
  5.2 8.0 %collective-permute-start.3 = (f32[56,128]{1,0:T(8,128)S(1)}, f32[56,128]{1,0:T(8,128)S(1)}, u32[]{:S(2)}, u32[]{:S(2)}) collective-permute-start(f32[56,128]{1,0:T(8,128)S(1)} %get-tuple-element.10), channel_id=1, source_target_pairs={{0,5},{1,4},{2,7},{3,6},{4,1},{5,0},{6,3},{7,2},{8,13},{9,12},{10,... | collective-permute-start | bytes 86024 | tf_op jit(solution)/shard_map/ppermute | solution.py:214
  7.9 4.0 %collective-permute-start.4 = (f32[16,128]{1,0:T(8,128)S(1)}, f32[16,128]{1,0:T(8,128)S(1)}, u32[]{:S(2)}, u32[]{:S(2)}) collective-permute-start(f32[16,128]{1,0:T(8,128)S(1)} %add.15), channel_id=1, source_target_pairs={{0,5},{1,4},{2,7},{3,6},{4,1},{5,0},{6,3},{7,2},{8,13},{9,12},{10,... | collective-permute-start | bytes 24584 | tf_op jit(solution)/shard_map/ppermute | solution.py:214
  9.3 5.4 %collective-permute-start.5 = (f32[72,128]{1,0:T(8,128)S(1)}, f32[72,128]{1,0:T(8,128)S(1)}, u32[]{:S(2)}, u32[]{:S(2)}) collective-permute-start(f32[72,128]{1,0:T(8,128)S(1)} %get-tuple-element.21), channel_id=1, source_target_pairs={{0,7},{1,6},{2,5},{3,4},{4,3},{5,2},{6,1},{7,0},{8,15},{9,14},{10,... | collective-permute-start | bytes 110600 | tf_op jit(solution)/shard_map/ppermute | solution.py:214
  11.6 4.7 %collective-permute-start.7 = (f32[72,128]{1,0:T(8,128)S(1)}, f32[72,128]{1,0:T(8,128)S(1)}, u32[]{:S(2)}, u32[]{:S(2)}) collective-permute-start(f32[72,128]{1,0:T(8,128)S(1)} %get-tuple-element.21), channel_id=1, source_target_pairs={{0,2},{1,3},{2,0},{3,1},{4,6},{5,7},{6,4},{7,5},{8,10},{9,11},{10,... | collective-permute-start | bytes 110600 | tf_op jit(solution)/shard_map/ppermute | solution.py:214
  11.9 4.3 %collective-permute-start.2 = (f32[72,128]{1,0:T(8,128)S(1)}, f32[72,128]{1,0:T(8,128)S(1)}, u32[]{:S(2)}, u32[]{:S(2)}) collective-permute-start(f32[72,128]{1,0:T(8,128)S(1)} %get-tuple-element.21), channel_id=1, source_target_pairs={{0,3},{1,2},{2,1},{3,0},{4,7},{5,6},{6,5},{7,4},{8,11},{9,10},{10,... | collective-permute-start | bytes 110600 | tf_op jit(solution)/shard_map/ppermute | solution.py:214
  14.7 1.6 %collective-permute-start.6 = (f32[3,72,128]{2,1,0:T(8,128)S(1)}, f32[3,72,128]{2,1,0:T(8,128)S(1)}, u32[]{:S(2)}, u32[]{:S(2)}) collective-permute-start(f32[3,72,128]{2,1,0:T(8,128)S(1)} %pad_maximum_fusion.2), channel_id=1, source_target_pairs={{0,1},{1,0},{2,3},{3,2},{4,5},{5,4},{6,7},{7,6},{8,9},{9,8},{10,11... | collective-permute-start | bytes 331784 | tf_op jit(solution)/shard_map/ppermute | solution.py:214
  17.8 5.8 %collective-permute-start.10 = (f32[1,18,128]{2,1,0:T(8,128)S(1)}, f32[1,18,128]{2,1,0:T(8,128)S(1)}, u32[]{:S(2)}, u32[]{:S(2)}) collective-permute-start(f32[1,18,128]{2,1,0:T(8,128)S(1)} %get-tuple-element.18), channel_id=1, source_target_pairs={{0,17},{1,16},{2,19},{3,18},{4,21},{5,20},{6,23},{7,22},{8,25},{9,... | collective-permute-start | bytes 27656 | tf_op jit(solution)/shard_map/ppermute | solution.py:214
  21.5 4.0 %collective-permute-start.11 = (f32[1,18,128]{2,1,0:T(8,128)S(1)}, f32[1,18,128]{2,1,0:T(8,128)S(1)}, u32[]{:S(2)}, u32[]{:S(2)}) collective-permute-start(f32[1,18,128]{2,1,0:T(8,128)S(1)} %get-tuple-element.17), channel_id=1, source_target_pairs={{0,25},{1,24},{2,27},{3,26},{4,29},{5,28},{6,31},{7,30},{8,17},{9,... | collective-permute-start | bytes 27656 | tf_op jit(solution)/shard_map/ppermute | solution.py:214
  21.7 3.8 %collective-permute-start.9 = (f32[1,18,128]{2,1,0:T(8,128)S(1)}, f32[1,18,128]{2,1,0:T(8,128)S(1)}, u32[]{:S(2)}, u32[]{:S(2)}) collective-permute-start(f32[1,18,128]{2,1,0:T(8,128)S(1)} %get-tuple-element.19), channel_id=1, source_target_pairs={{0,9},{1,8},{2,11},{3,10},{4,13},{5,12},{6,15},{7,14},{8,1},{9,0},... | collective-permute-start | bytes 27656 | tf_op jit(solution)/shard_map/ppermute | solution.py:214
